TPU v7x, 32 devices: a whole 2x2x4 slice. The times are simulated.
32 devices in a mesh: facet: 8 (over y, x, core), pulse: 4 (over z).
Axes of the slice: x: 2, y: 2, z: 4, core: 2. Of those that a mesh axis runs over, the one named last changes fastest.
Arguments:
- facet_positions: float32 [3, 6144], P(None, 'facet'), may hold values from -10 to 10
- reflectivity: float32 [2, 6144], P(None, 'facet'), may hold values from -0.109375 to 0.109375
- block_building: int32 [48], P('facet'), may hold values from 0 to 11, never falling along the last dimension, each value on 1 to 8 neighbouring positions
- visible: int32 [12, 64], P(None, 'pulse'), may hold values from 0 to 1
- platform: float32 [3, 2048], P(None, 'pulse'), may hold values from 30 to 40
Outputs:
- image: float32 [2, 512, 2048], P(None, 'pulse', 'facet')
All inputs are finite; a program needn't handle non-finite values.
Results may differ from a plain program's by a relative error of at most 0.017.
Values may be sent and summed in bfloat16 or wider, within the bound.
No kernel may reach another device: no remote copies, remote signals or barrier semaphores. Data moves between devices by JAX's collectives and lax.ppermute only.
A program may use at most 64 MiB of HBM per device.

v0:
```python
import functools
import math

import jax
import jax.numpy as jnp
import numpy as np
from jax import lax
from jax.experimental import pallas as pl
from jax.experimental.pallas import tpu as pltpu
from jax.sharding import PartitionSpec as P


BLK = 128
PBS = 32
BINS = 512
LANES = 128
STEP = 4
QUADS = 4


f32 = jnp.float32
bf16 = jnp.bfloat16

SIN_C = (4.442882878126042, -7.308239958462742, 3.606233657443361, -0.8453187380162854, 0.10822102663962477)
COS_C = (-1.4142135611352313, 6.978863916510845, -5.739875235214542, 1.8882041596407644, -0.33193097868538995, 0.03399741622323665)


def poly(coefs, w):
    acc = w * coefs[-1] + coefs[-2]
    for c in coefs[-3::-1]:
        acc = acc * w + c
    return acc


def cis_turns(v):
    w = v * v
    s = v * poly(SIN_C, w)
    c = poly(COS_C, w)
    return 1.0 - s * s, -(s * c)


def fold_matrix():
    left = np.zeros((8, 2, 4))
    for m in range(2):
        plus, minus = (2 + m, 1 - m)
        for which, (c, sign) in enumerate(((0, 1), (0, 1), (1, 1), (1, -1))):
            left[m * 4 + which, c, plus] = sign
            left[m * 4 + which, c, minus] = (sign, -sign)[which % 2]
    right = np.zeros((16, 2, 2, 16))
    for mp in range(2):
        for m in range(2):
            for low in range(2):
                middle, off = 4 + 8 * (2 * mp + low), (1, 3)[m]
                for which, (cs, plus, minus) in enumerate(((0, 1, 1), (0, -1, 1), (1, 1, 1), (1, 1, -1))):
                    right[mp * 8 + m * 4 + which, low, cs, (middle + off - 1) // 2] = plus
                    right[mp * 8 + m * 4 + which, low, cs, (middle - off - 1) // 2] = minus
    both = np.einsum("tca,ulsj->tulcsaj", left, right)
    out = np.zeros((8, 16, 2, 2, 4, 32))
    up, down = slice(16, 32), slice(15, None, -1)
    out[:, :, :, 0, :, up] = both[:, :, :, 0, 0] + both[:, :, :, 1, 1]
    out[:, :, :, 0, :, down] = both[:, :, :, 0, 0] - both[:, :, :, 1, 1]
    out[:, :, :, 1, :, up] = both[:, :, :, 1, 0] - both[:, :, :, 0, 1]
    out[:, :, :, 1, :, down] = both[:, :, :, 1, 0] + both[:, :, :, 0, 1]
    return out.reshape(8 * 32, 2 * 4 * 32) / 16.0


def pack(low, high):
    return jnp.concatenate([low, high], axis=0).astype(bf16)


def block_angles(x, y, z, ax, ay, az):
    dx, dy, dz = x - ax, y - ay, z - az
    d2 = dx * dx + dy * dy + dz * dz
    t = d2 * lax.rsqrt(d2) - 1.25
    w = t * t
    s = t * poly(SIN_C, w)
    return s * poly(COS_C, w), 1.0 - s * s


def block_factors(c1, s1, r0, r1):
    square = c1 * c1
    a2, b2 = 4.0 * square - 2.0, 4.0 * (c1 * s1)
    c3, s3 = (a2 - 1.0) * c1, (a2 + 1.0) * s1
    a4, b4 = a2 * a2 - 2.0, a2 * b2
    a8, b8 = a4 * a4 - 2.0, a4 * b4
    a12, b12 = (a8 - 1.0) * a4, (a8 + 1.0) * b4
    a20, b20 = a8 * a12 - a4, a8 * b12 - b4
    a28, b28 = a8 * a20 - a12, a8 * b20 - b12
    a16, b16 = a8 * a8 - 2.0, a8 * b8
    a32, b32 = a16 * a16 - 2.0, a16 * b16
    a64, b64 = a32 * a32 - 2.0, a32 * b32
    a128, b128 = a64 * a64 - 2.0, a64 * b64
    a256, b256 = a128 * a128 - 2.0, a128 * b128
    a96, b96 = (a64 - 1.0) * a32, (a64 + 1.0) * b32
    c256, s256 = 0.5 * a256, 0.5 * b256
    c144, s144 = a128 * a16 - b128 * b16, b128 * a16 + a128 * b16
    c143, s143 = c144 * c1 + s144 * s1, s144 * c1 - c144 * s1
    q0r, q0i = r0 * c143 + r1 * s143, r1 * c143 - r0 * s143
    q1r, q1i = q0r * c256 + q0i * s256, q0i * c256 - q0r * s256
    q2r, q2i = a256 * q1r - q0r, a256 * q1i - q0i
    q3r, q3i = a256 * q2r - q1r, a256 * q2i - q1i
    return (
        a32, b32, a96, b96, q0r, q0i, q1r, q1i, q2r, q2i, q3r, q3i,
        c1, s1, c3, s3, a4, b4, a12, b12, a20, b20, a28, b28,
    )


def table_of(factors):
    near, far = factors[:4], factors[4:]
    near = [pack(value, value) for value in near]
    tiles = []
    for low in (0, 4):
        real, imag = pack(far[low], far[low + 2]), pack(far[low + 1], far[low + 3])
        for cosine, sine in (near[0:2], near[2:4]):
            tiles += [real * cosine, imag * sine, imag * cosine, real * sine]
    return jnp.concatenate(tiles, axis=0)


def echo_kernel(
    pieces, blocks, groups, group_len, buildings,
    platform_ref, fold, *refs,
):
    piece_refs = refs[:pieces]
    out_ref, fac_ref, marks_v, marks_s, rows_s, antenna, angles, products, sem = refs[pieces:]
    mine = lax.axis_index("facet")
    in_turns = 1.0 / (16.0 * math.pi)
    scale = jnp.where(lax.broadcasted_iota(jnp.int32, (8, LANES), 0) < 3, in_turns, 1.0)
    for piece, ref in enumerate(piece_refs):
        for j in range(blocks):
            at = (piece * blocks + j) * 8
            fac_ref[at : at + 8, :] = ref[:, j * LANES : j * LANES + LANES] * scale
    fac_ref[pieces * blocks * 8 :, :] = jnp.zeros((8, LANES), f32)
    ids = jnp.concatenate([ref[5:6, :LANES] for ref in piece_refs], axis=0)
    marks = jnp.zeros(ids.shape, jnp.int32)
    for b in range(buildings):
        marks = jnp.where(ids == float(b), piece_refs[0][6:7, b : b + 1].astype(jnp.int32), marks)
    marks_v[:pieces, :] = marks
    marks_v[pieces:, :] = jnp.zeros((8, LANES), jnp.int32)
    marks_copy = pltpu.make_async_copy(marks_v, marks_s, sem)
    marks_copy.start()
    pulse_dev = platform_ref.shape[1]
    flat = platform_ref[...] * in_turns
    flat = jnp.concatenate([flat, jnp.zeros((8 - flat.shape[0], pulse_dev), f32)], axis=0)
    antenna[:pulse_dev, :8] = flat.T
    antenna[pulse_dev:, :] = jnp.zeros((8, LANES), f32)
    marks_copy.wait()
    most = pieces * blocks + 3 * STEP

    def scan(piece, g, at):
        for j in range(blocks):
            rows_s[at] = (piece * blocks + j) * 8
            at = at + (lax.shift_right_logical(marks_s[piece, j], g) & 1)
        return at

    def close(at):
        for extra in range(3 * STEP):
            rows_s[at + extra] = pieces * blocks * 8

    def station(g):
        g = jnp.minimum(g, groups - 1)
        ant = antenna[pl.ds((g * pieces + mine) * group_len, 8), :]
        return [jnp.broadcast_to(ant[:, i : i + 1], (8, LANES)) for i in range(3)]

    def turn(at, place):
        for j in range(STEP):
            row = rows_s[at + j]
            facet = [fac_ref[pl.ds(row + c, 8, stride=0), :] for c in range(3)]
            angles[j, 0], angles[j, 1] = block_angles(*facet, *place)

    def read(at, j):
        row = rows_s[at + j]
        weights = [fac_ref[pl.ds(row + c, 8, stride=0), :] for c in (3, 4)]
        return angles[j, 0], angles[j, 1], *weights

    same = (
        lax.broadcasted_iota(jnp.int32, (16, 256), 0) % 8
        == lax.broadcasted_iota(jnp.int32, (16, 256), 1) % 8
    )

    def group(acc0, acc1, g, count):
        place = station(g)
        here, there = (g % 2) * most, ((g + 1) % 2) * most
        steps = jnp.maximum(lax.div(count + (STEP - 1), STEP), 1)

        def step(i, at):
            for half, acc in ((0, acc0), (1, acc1)):
                pair = [block_factors(*read(here + i * STEP, 2 * half + j)) for j in range(2)]
                right = jnp.concatenate([table_of(p[12:]) for p in pair], axis=1)
                left = jnp.concatenate([table_of(p[:12]) for p in pair], axis=1)
                pltpu.matmul_push_rhs(right, staging_register=0, mxu_index=half, transpose=True)
                pltpu.matmul_acc_lhs(acc, left, load_staged_rhs=0)
            turn(here + (i + 1) * STEP, place)
            return scan(jnp.minimum(i, pieces), g + 1, at)

        at = lax.fori_loop(0, steps, step, there)
        at = lax.fori_loop(
            jnp.minimum(steps, pieces), pieces, lambda piece, n: scan(piece, g + 1, n), at
        )
        close(at)
        turn(there, station(g + 1))
        total = pltpu.matmul_pop(acc0) + pltpu.matmul_pop(acc1)
        for tile in range(16):
            hp, spot = tile // 8, tile % 8
            kept = jnp.where(same, total[tile * 16 : tile * 16 + 16, :], 0.0).astype(bf16)
            products[hp, pl.ds(pl.multiple_of(g * 16, 16), 16), spot * 256 : spot * 256 + 256] = kept
        return at - there

    first = lax.fori_loop(0, pieces, lambda piece, n: scan(piece, 0, n), jnp.int32(0))
    close(first)
    turn(0, station(0))
    pl.run_scoped(
        lambda acc0, acc1: lax.fori_loop(0, groups, functools.partial(group, acc0, acc1), first),
        pltpu.ACC(0)((256, 256), f32), pltpu.ACC(1)((256, 256), f32),
    )
    pl.run_scoped(
        functools.partial(fold_products, groups, products, fold, out_ref),
        pltpu.ACC(0)((groups * 16, 256), f32), pltpu.ACC(1)((groups * 16, 256), f32),
    )


def fold_products(groups, products, fold, out_ref, *accs):
    for k in range(8):
        lanes = slice(k * 256, k * 256 + 256)
        for hp, acc in enumerate(accs):
            pltpu.matmul_push_rhs(fold[lanes, :], staging_register=k % 2, mxu_index=hp)
            pltpu.matmul_acc_lhs(acc, products[hp, :, lanes], load_staged_rhs=k % 2)
    for hp, acc in enumerate(accs):
        echo = pltpu.matmul_pop(acc)
        for low in range(2):
            picked = [echo[g * 16 + low * 8 : g * 16 + low * 8 + 8] for g in range(groups)]
            out_ref[2 * hp + low] = jnp.concatenate(picked, axis=0).astype(bf16)


def echoes(buildings, platform, fold, facets, blocks, groups, group_len):
    pieces = len(facets)
    most = pieces * blocks + 3 * STEP
    pulse_dev = platform.shape[1]
    vmem = pl.BlockSpec(memory_space=pltpu.VMEM)
    return pl.pallas_call(
        functools.partial(echo_kernel, pieces, blocks, groups, group_len, buildings),
        out_shape=jax.ShapeDtypeStruct((QUADS, groups * 8, 256), bf16),
        in_specs=[vmem] * (2 + pieces),
        out_specs=vmem,
        scratch_shapes=[
            pltpu.VMEM(((pieces * blocks + 1) * 8, LANES), f32),
            pltpu.VMEM((pieces + 8, LANES), jnp.int32),
            pltpu.SMEM((pieces + 8, LANES), jnp.int32),
            pltpu.SMEM((2 * most + 3 * STEP,), jnp.int32),
            pltpu.VMEM((pulse_dev + 8, LANES), f32),
            pltpu.VMEM((STEP, 2, 8, LANES), f32),
            pltpu.VMEM((2, groups * 16, 2048), bf16),
            pltpu.SemaphoreType.DMA,
        ],
        compiler_params=pltpu.CompilerParams(vmem_limit_bytes=16 << 20),
        name="echoes",
    )(platform, fold, *facets)


def pack_kernel(
    groups, group_len, ids_hbm, positions_hbm, reflectivity_hbm, visible_hbm, platform_hbm,
    out_ref, stations_ref, ids, positions, reflectivity, visible, sems,
):
    mine, count = lax.axis_index("facet"), lax.axis_size("facet")
    copies = [
        pltpu.make_async_copy(source, target, sems.at[i])
        for i, (source, target) in enumerate((
            (visible_hbm, visible), (ids_hbm, ids),
            (positions_hbm, positions), (reflectivity_hbm, reflectivity), (platform_hbm, stations_ref),
        ))
    ]
    for copy in copies:
        copy.start()
    for copy in copies[:2]:
        copy.wait()
    lane = lax.broadcasted_iota(jnp.int32, (1, LANES), 1)
    row = jnp.zeros(lane.shape, f32)
    for j in range(ids.shape[0]):
        row = jnp.where(lane == j, ids[j].astype(f32), row)
    words = jnp.zeros(lane.shape, jnp.int32)
    columns = [lax.div((g * count + mine) * group_len, PBS) for g in range(groups)]
    for b in range(visible.shape[0]):
        word = jnp.int32(0)
        for g, column in enumerate(columns):
            word = word | lax.shift_left(visible[b, column], g)
        words = jnp.where(lane == b, word, words)
    for copy in copies[2:]:
        copy.wait()
    out_ref[0:3, :] = positions[...]
    out_ref[3:5, :] = reflectivity[...]
    out_ref[5:8, :LANES] = jnp.concatenate([row, words.astype(f32), jnp.zeros_like(row)], axis=0)
    out_ref[5:8, LANES:] = jnp.zeros((3, out_ref.shape[1] - LANES), f32)


def in_hbm(x):
    return pltpu.with_memory_space_constraint(x, pltpu.HBM)


def pack_facets(ids, positions, reflectivity, visible, platform, groups, group_len):
    vmem = pl.BlockSpec(memory_space=pltpu.VMEM)
    return pl.pallas_call(
        functools.partial(pack_kernel, groups, group_len),
        out_shape=(
            jax.ShapeDtypeStruct((8, positions.shape[1]), f32),
            jax.ShapeDtypeStruct(platform.shape, f32),
        ),
        in_specs=[pl.BlockSpec(memory_space=pltpu.HBM)] * 5,
        out_specs=(vmem, vmem),
        scratch_shapes=[
            pltpu.SMEM(ids.shape, jnp.int32),
            pltpu.VMEM(positions.shape, f32),
            pltpu.VMEM(reflectivity.shape, f32),
            pltpu.SMEM(visible.shape, jnp.int32),
            pltpu.SemaphoreType.DMA((5,)),
        ],
        compiler_params=pltpu.CompilerParams(vmem_limit_bytes=4 << 20),
        name="pack_facets",
    )(*map(in_hbm, (ids, positions, reflectivity, visible, platform)))


def transform_tables_kernel(
    facet_n, pulse_n, order, share, group_len, pulses, bins_dev, k_block,
    after_ref, w_ref, chirp_ref,
):
    mine_f, mine_z = lax.axis_index("facet"), lax.axis_index("pulse")
    k_ids = mine_f * k_block + lax.broadcasted_iota(jnp.int32, (k_block, LANES), 0)
    lane = lax.broadcasted_iota(jnp.int32, (k_block, LANES), 1)
    pulse_dev = pulses // pulse_n

    def rotation(index):
        back = (index + pulses // 2) % pulses - pulses // 2
        cosine, sine = cis_turns(back.astype(f32) * (1.0 / pulses))
        return cosine, -sine

    slot = lane // share
    within = lane % share
    here = (mine_z ^ (slot % pulse_n)) * pulse_dev + (
        within // group_len * facet_n + mine_f
    ) * group_len + within % group_len
    scale = 1.0 / math.sqrt(pulses)
    real, imag = rotation((k_ids * here) % pulses)
    wide = {0: (real * scale, imag * scale)}
    per_block = LANES // share
    turns = []
    bit = 1
    while bit < pulse_n:
        if bit >= per_block:
            sign = 1 - 2 * ((mine_z // bit) % 2)
            turns.append(sign * pulse_dev * bit)
        bit *= 2
    for bit in order:
        sign = 1 - 2 * ((mine_f // bit) % 2)
        turns.append(sign * group_len * bit)
    for level, turn in enumerate(turns):
        rr, ri = rotation((k_ids * turn) % pulses)
        for at in range(1 << level):
            real, imag = wide[at]
            wide[at + (1 << level)] = (real * rr - imag * ri, real * ri + imag * rr)
    for at, (real, imag) in wide.items():
        w_ref[:k_block, at * LANES : at * LANES + LANES] = real.astype(bf16)
        w_ref[k_block:, at * LANES : at * LANES + LANES] = imag.astype(bf16)
    offset = mine_f * k_block - pulses // 2 + lax.broadcasted_iota(jnp.int32, (k_block, bins_dev), 0)
    bins = mine_z * bins_dev + lax.broadcasted_iota(jnp.int32, (k_block, bins_dev), 1)
    phase = (offset * offset).astype(f32) * (8.0 / (2.0 * pulses)) / (8.0 + bins.astype(f32))
    cosine, sine = cis_turns(phase - jnp.round(phase))
    chirp_ref[0] = cosine
    chirp_ref[1] = sine


def transform_tables(after, facet_n, pulse_n, order, share, group_len, pulses, bins_dev, k_block):
    return pl.pallas_call(
        functools.partial(
            transform_tables_kernel, facet_n, pulse_n, order, share, group_len, pulses, bins_dev, k_block
        ),
        out_shape=(
            jax.ShapeDtypeStruct((2 * k_block, pulses), bf16),
            jax.ShapeDtypeStruct((2, k_block, bins_dev), f32),
        ),
        in_specs=[pl.BlockSpec(memory_space=pl.ANY)],
        out_specs=(pl.BlockSpec(memory_space=pltpu.VMEM),) * 2,
        compiler_params=pltpu.CompilerParams(vmem_limit_bytes=16 << 20),
        name="transform_tables",
    )(after)


def transform_kernel(places, has_total, k_block, bins_dev, w_ref, *refs):
    total = refs[0][...] if has_total else None
    pieces = refs[has_total : has_total + len(places)]
    for place, piece in zip(places, pieces):
        rows = piece.shape[0]
        part = jnp.dot(
            w_ref[:, place * rows : place * rows + rows], piece[...], preferred_element_type=f32
        )
        total = part if total is None else total + part
    rest = refs[has_total + len(places) :]
    if len(rest) == 1:
        rest[0][...] = total
        return
    chirp_ref, out_ref = rest
    real = total[:k_block, :bins_dev] - total[k_block:, bins_dev:]
    imag = total[k_block:, :bins_dev] + total[:k_block, bins_dev:]
    cosine, sine = chirp_ref[0], chirp_ref[1]
    out_ref[0] = (cosine * real - sine * imag).T
    out_ref[1] = (cosine * imag + sine * real).T


def transform(w, total, pieces, places, k_block, bins_dev, chirp=None):
    operands = [w] + ([] if total is None else [total]) + [pieces[at] for at in places]
    shape = (2 * k_block, 2 * bins_dev)
    if chirp is not None:
        operands.append(chirp)
        shape = (2, bins_dev, k_block)
    vmem = pl.BlockSpec(memory_space=pltpu.VMEM)
    return pl.pallas_call(
        functools.partial(transform_kernel, places, total is not None, k_block, bins_dev),
        out_shape=jax.ShapeDtypeStruct(shape, f32),
        in_specs=[vmem] * len(operands),
        out_specs=vmem,
        compiler_params=pltpu.CompilerParams(vmem_limit_bytes=16 << 20),
        name="transform",
    )(*operands)


def swap(x, axis, size, mask):
    return lax.ppermute(x, axis, [(i, i ^ mask) for i in range(size)])


def gather_facet(x, size):
    near = [x]
    for mask in range(2, size, 2):
        near.append(swap(x, "facet", size, mask))
    out = []
    for mask, piece in zip(range(0, size, 2), near):
        out += [piece, swap(piece, "facet", size, 1)]
    return out


def body(facet_positions, reflectivity, block_building, visible, platform):
    facet_n = lax.axis_size("facet")
    pulse_n = lax.axis_size("pulse")
    mine_z = lax.axis_index("pulse")
    pulse_dev = platform.shape[1]
    pulses = pulse_dev * pulse_n
    blocks = facet_positions.shape[1] // BLK
    share = pulse_dev // facet_n
    group_len = min(8, share)
    groups = share // group_len
    bins_dev = BINS // pulse_n
    k_block = pulses // facet_n
    buildings = visible.shape[0]

    packed, stations = pack_facets(
        block_building, facet_positions, reflectivity, visible, platform, groups, group_len
    )
    facets = gather_facet(packed, facet_n)

    one = (lax.axis_index("facet") >= 0).astype(bf16)
    fold = jnp.broadcast_to(jnp.asarray(fold_matrix(), bf16)[:, None, :], (256, 8, 256)) * one
    fold = fold.reshape(2048, 256)
    echo = echoes(buildings, stations, fold, facets, blocks, groups, group_len)
    order = [1 << i for i in range(facet_n.bit_length() - 1)]
    w, chirp = transform_tables(
        echo, facet_n, pulse_n, order, share, group_len, pulses, bins_dev, k_block
    )

    echo = echo.reshape(QUADS, groups, 8, 2, LANES)[:, :, :group_len]
    if pulse_n > QUADS:
        echo = echo.reshape(QUADS, share, 2, pulse_n // QUADS, bins_dev).transpose(0, 3, 1, 2, 4)
    echo = echo.reshape(pulse_n, share, 2 * bins_dev)
    turned = [lax.dynamic_index_in_dim(echo, mine_z, 0, keepdims=False)]
    for mask in range(1, pulse_n):
        piece = lax.dynamic_index_in_dim(echo, mine_z ^ mask, 0, keepdims=False)
        turned.append(swap(piece, "pulse", pulse_n, mask))
    turned, w, chirp = lax.optimization_barrier((jnp.concatenate(turned), w, chirp))

    pieces = gather_facet(turned, facet_n)
    total = transform(w, None, pieces, [0, 1], k_block, bins_dev)
    total = transform(w, total, pieces, list(range(2, facet_n, 2)), k_block, bins_dev)
    return transform(w, total, pieces, list(range(3, facet_n, 2)), k_block, bins_dev, chirp)


def solution(mesh):
    placed = (P(None, "facet"), P(None, "facet"), P("facet"), P(None, "pulse"), P(None, "pulse"))
    return jax.shard_map(body, mesh=mesh, in_specs=placed, out_specs=P(None, "pulse", "facet"), check_vma=False)
```

profile of v0, /device:TPU:0, one launch (start us, length us, event | category | flops | bytes accessed | tf_op | source)
XLA Modules:
  0.0 47.1 jit_solution(18004237901581857844)
XLA Ops:
  0.0 1.0 %pack_facets.1 = (f32[8,768]{1,0:T(8,128)S(1)}, f32[3,512]{1,0:T(4,128)S(1)}) custom-call(s32[6]{0:T(128)} %ids_hbm.1, f32[3,768]{1,0:T(4,128)} %positions_hbm.1, f32[2,768]{1,0:T(2,128)} %reflectivity_hbm.1, s32[12,16]{1,0:T(8,128)} %visible_hbm.1, f32[3,512]{1,0:T(4,128)} %platform_hbm.1), custom_call_target="tpu_custom_call" | custom-call | tf_op jit(solution)/shard_map/pack_facets/pallas_call | solution.py:300
  1.0 3.0 %collective-permute-start.1 = (f32[8,768]{1,0:T(8,128)S(1)}, f32[8,768]{1,0:T(8,128)S(1)}, u32[]{:S(2)}, u32[]{:S(2)}) collective-permute-start(f32[8,768]{1,0:T(8,128)S(1)} %get-tuple-element.13.refs_0_), channel_id=1, source_target_pairs={{0,8},{4,12},{8,0},{12,4},{16,24},{20,28},{24,16},{28,20},{1,9},{5... | collective-permute-start | bytes 73736 | tf_op jit(solution)/shard_map/ppermute | solution.py:424
  4.1 1.5 %collective-permute-start.3 = (f32[8,768]{1,0:T(8,128)S(1)}, f32[8,768]{1,0:T(8,128)S(1)}, u32[]{:S(2)}, u32[]{:S(2)}) collective-permute-start(f32[8,768]{1,0:T(8,128)S(1)} %get-tuple-element.13.refs_0_), channel_id=1, source_target_pairs={{0,16},{4,20},{8,24},{12,28},{16,0},{20,4},{24,8},{28,12},{1,17},{... | collective-permute-start | bytes 73736 | tf_op jit(solution)/shard_map/ppermute | solution.py:424
  5.6 0.0 collective-permute-start.5
  5.6 0.0 collective-permute-start
  5.6 0.9 %broadcast_multiply_fusion = bf16[256,256]{1,0:T(8,128)(2,1)S(1)} fusion(bf16[256,256]{1,0:T(8,128)(2,1)} %constant.30.clone, bf16[]{:T(256)S(6)} %convert_element_type.3), kind=kLoop, calls=%fused_computation.2 | loop fusion | flops 65536 | bytes 262146 | tf_op jit(solution)/shard_map/mul | solution.py:457
  6.5 0.0 collective-permute-done.1.refs_2_
  6.5 0.6 %collective-permute-start.2 = (f32[8,768]{1,0:T(8,128)S(1)}, f32[8,768]{1,0:T(8,128)S(1)}, u32[]{:S(2)}, u32[]{:S(2)}) collective-permute-start(f32[8,768]{1,0:T(8,128)S(1)} %collective-permute-done.1.refs_2_), channel_id=1, source_target_pairs={{0,4},{4,0},{8,12},{12,8},{16,20},{20,16},{24,28},{28,24},{1,5},{5... | collective-permute-start | bytes 73736 | tf_op jit(solution)/shard_map/ppermute | solution.py:424
  7.1 0.8 %collective-permute-done.3.refs_4_ = f32[8,768]{1,0:T(8,128)S(1)} collective-permute-done((f32[8,768]{1,0:T(8,128)S(1)}, f32[8,768]{1,0:T(8,128)S(1)}, u32[]{:S(2)}, u32[]{:S(2)}) %collective-permute-start.3) | collective-permute-done | bytes 24608 | tf_op jit(solution)/shard_map/ppermute | solution.py:424
  7.9 0.0 collective-permute-start.4
  7.9 2.4 %collective-permute-done.5.refs_6_ = f32[8,768]{1,0:T(8,128)S(1)} collective-permute-done((f32[8,768]{1,0:T(8,128)S(1)}, f32[8,768]{1,0:T(8,128)S(1)}, u32[]{:S(2)}, u32[]{:S(2)}) %collective-permute-start.5) | collective-permute-done | bytes 24608 | tf_op jit(solution)/shard_map/ppermute | solution.py:424
  10.3 0.0 collective-permute-start.6
  10.3 0.1 broadcast_bitcast_fusion.fold
  10.5 0.0 collective-permute-done.refs_1_
  10.5 0.0 collective-permute-done.2.refs_3_
  10.5 0.0 collective-permute-done.4.refs_5_
  10.5 1.0 %collective-permute-done.6.refs_7_ = f32[8,768]{1,0:T(8,128)S(1)} collective-permute-done((f32[8,768]{1,0:T(8,128)S(1)}, f32[8,768]{1,0:T(8,128)S(1)}, u32[]{:S(2)}, u32[]{:S(2)}) %collective-permute-start.6) | collective-permute-done | bytes 24608 | tf_op jit(solution)/shard_map/ppermute | solution.py:424
  11.5 14.3 %echoes.1.after_ref = bf16[4,64,256]{2,1,0:T(8,128)(2,1)S(1)} custom-call(f32[3,512]{1,0:T(4,128)S(1)} %get-tuple-element.12.platform_ref, bf16[2048,256]{1,0:T(8,128)(2,1)S(1)} %broadcast_bitcast_fusion.fold, f32[8,768]{1,0:T(8,128)S(1)} %get-tuple-element.13.refs_0_, f32[8,768]{1,0:T(8,128)S(1)} %collective-permute-done.refs_1_, ...), custom_call_target="tpu_custom_call" | custom-call | tf_op jit(solution)/shard_map/echoes/pallas_call | solution.py:239
  25.9 5.4 %collective-permute-start.7 = (bf16[64,256]{1,0:T(8,128)(2,1)S(1)}, bf16[64,256]{1,0:T(8,128)(2,1)S(1)}, u32[]{:S(2)}, u32[]{:S(2)}) collective-permute-start(bf16[64,256]{1,0:T(8,128)(2,1)S(1)} %get-tuple-element.22), channel_id=1, source_target_pairs={{0,1},{1,0},{2,3},{3,2},{4,5},{5,4},{6,7},{7,6},{8,9},{9,8},{10,11... | collective-permute-start | bytes 98312 | tf_op jit(solution)/shard_map/ppermute | solution.py:424
  31.3 0.4 collective-permute-start.8
  31.7 2.0 %collective-permute-start.9 = (bf16[64,256]{1,0:T(8,128)(2,1)S(1)}, bf16[64,256]{1,0:T(8,128)(2,1)S(1)}, u32[]{:S(2)}, u32[]{:S(2)}) collective-permute-start(bf16[64,256]{1,0:T(8,128)(2,1)S(1)} %get-tuple-element.20), channel_id=1, source_target_pairs={{0,3},{1,2},{2,1},{3,0},{4,7},{5,6},{6,5},{7,4},{8,11},{9,10},{10,... | collective-permute-start | bytes 98312 | tf_op jit(solution)/shard_map/ppermute | solution.py:424
  33.7 2.0 %transform_tables.1 = (bf16[512,2048]{1,0:T(8,128)(2,1)S(1)}, f32[2,256,128]{2,1,0:T(8,128)S(1)}) custom-call(bf16[4,64,256]{2,1,0:T(8,128)(2,1)S(1)} %echoes.1.after_ref), custom_call_target="tpu_custom_call" | custom-call | tf_op jit(solution)/shard_map/transform_tables/pallas_call | solution.py:370
  35.7 0.0 collective-permute-done.7
  35.7 0.8 %collective-permute-done.8 = bf16[64,256]{1,0:T(8,128)(2,1)S(1)} collective-permute-done((bf16[64,256]{1,0:T(8,128)(2,1)S(1)}, bf16[64,256]{1,0:T(8,128)(2,1)S(1)}, u32[]{:S(2)}, u32[]{:S(2)}) %collective-permute-start.8) | collective-permute-done | bytes 32800 | tf_op jit(solution)/shard_map/ppermute | solution.py:424
  36.5 0.9 %collective-permute-done.9 = bf16[64,256]{1,0:T(8,128)(2,1)S(1)} collective-permute-done((bf16[64,256]{1,0:T(8,128)(2,1)S(1)}, bf16[64,256]{1,0:T(8,128)(2,1)S(1)}, u32[]{:S(2)}, u32[]{:S(2)}) %collective-permute-start.9) | collective-permute-done | bytes 32800 | tf_op jit(solution)/shard_map/ppermute | solution.py:424
  37.4 0.5 %collective-permute-start.11 = (bf16[256,256]{1,0:T(8,128)(2,1)S(1)}, bf16[256,256]{1,0:T(8,128)(2,1)S(1)}, u32[]{:S(2)}, u32[]{:S(2)}) collective-permute-start(bf16[256,256]{1,0:T(8,128)(2,1)S(1)} %pad_maximum_fusion.refs_0_), channel_id=1, source_target_pairs={{0,8},{4,12},{8,0},{12,4},{16,24},{20,28},{24,16},{28,20},{1,9},{5... | collective-permute-start | bytes 393224 | tf_op jit(solution)/shard_map/ppermute | solution.py:424
  37.9 0.1 collective-permute-start.12
  38.1 2.9 %collective-permute-start.13 = (bf16[256,256]{1,0:T(8,128)(2,1)S(1)}, bf16[256,256]{1,0:T(8,128)(2,1)S(1)}, u32[]{:S(2)}, u32[]{:S(2)}) collective-permute-start(bf16[256,256]{1,0:T(8,128)(2,1)S(1)} %pad_maximum_fusion.refs_0_), channel_id=1, source_target_pairs={{0,24},{4,28},{8,16},{12,20},{16,8},{20,12},{24,0},{28,4},{1,25},{... | collective-permute-start | bytes 393224 | tf_op jit(solution)/shard_map/ppermute | solution.py:424
  41.0 0.0 collective-permute-start.10
  41.0 1.8 %collective-permute-done.11.refs_1_ = bf16[256,256]{1,0:T(8,128)(2,1)S(1)} collective-permute-done((bf16[256,256]{1,0:T(8,128)(2,1)S(1)}, bf16[256,256]{1,0:T(8,128)(2,1)S(1)}, u32[]{:S(2)}, u32[]{:S(2)}) %collective-permute-start.11) | collective-permute-done | bytes 131104 | tf_op jit(solution)/shard_map/ppermute | solution.py:424
  42.8 0.0 collective-permute-start.14
  42.8 1.6 %collective-permute-done.12.refs_2_ = bf16[256,256]{1,0:T(8,128)(2,1)S(1)} collective-permute-done((bf16[256,256]{1,0:T(8,128)(2,1)S(1)}, bf16[256,256]{1,0:T(8,128)(2,1)S(1)}, u32[]{:S(2)}, u32[]{:S(2)}) %collective-permute-start.12) | collective-permute-done | bytes 131104 | tf_op jit(solution)/shard_map/ppermute | solution.py:424
  44.4 0.0 collective-permute-start.15
  44.4 0.0 collective-permute-done.13.refs_3_
  44.4 0.5 %collective-permute-start.16 = (bf16[256,256]{1,0:T(8,128)(2,1)S(1)}, bf16[256,256]{1,0:T(8,128)(2,1)S(1)}, u32[]{:S(2)}, u32[]{:S(2)}) collective-permute-start(bf16[256,256]{1,0:T(8,128)(2,1)S(1)} %collective-permute-done.13.refs_3_), channel_id=1, source_target_pairs={{0,4},{4,0},{8,12},{12,8},{16,20},{20,16},{24,28},{28,24},{1,5},{5... | collective-permute-start | bytes 393224 | tf_op jit(solution)/shard_map/ppermute | solution.py:424
  44.9 0.0 collective-permute-done.10.refs_1_
  44.9 0.3 transform.3.refs_0_
  45.2 0.4 transform.4.refs_0_
  45.6 0.0 collective-permute-done.14.refs_1_
  45.6 0.1 collective-permute-done.15.refs_2_
  45.8 0.2 collective-permute-done.16.refs_3_
  45.9 1.2 %transform.5 = f32[2,128,256]{2,1,0:T(8,128)} custom-call(bf16[512,2048]{1,0:T(8,128)(2,1)S(1)} %get-tuple-element.16.w_ref, f32[512,256]{1,0:T(8,128)S(1)} %transform.4.refs_0_, bf16[256,256]{1,0:T(8,128)(2,1)S(1)} %collective-permute-done.14.refs_1_, bf16[256,256]{1,0:T(8,128)(2,1)S(1)} %collective-permute-done.15.refs_2_, ...), custom_call_target="tpu_custom_call" | custom-call | tf_op jit(solution)/shard_map/transform/pallas_call | solution.py:413
  (2 shorter events, 0.0 us)
Async XLA Ops:
  1.0 5.5 %collective-permute-start.1 = (f32[8,768]{1,0:T(8,128)S(1)}, f32[8,768]{1,0:T(8,128)S(1)}, u32[]{:S(2)}, u32[]{:S(2)}) collective-permute-start(f32[8,768]{1,0:T(8,128)S(1)} %get-tuple-element.13.refs_0_), channel_id=1, source_target_pairs={{0,8},{4,12},{8,0},{12,4},{16,24},{20,28},{24,16},{28,20},{1,9},{5... | collective-permute-start | bytes 73736 | tf_op jit(solution)/shard_map/ppermute | solution.py:424
  4.1 3.8 %collective-permute-start.3 = (f32[8,768]{1,0:T(8,128)S(1)}, f32[8,768]{1,0:T(8,128)S(1)}, u32[]{:S(2)}, u32[]{:S(2)}) collective-permute-start(f32[8,768]{1,0:T(8,128)S(1)} %get-tuple-element.13.refs_0_), channel_id=1, source_target_pairs={{0,16},{4,20},{8,24},{12,28},{16,0},{20,4},{24,8},{28,12},{1,17},{... | collective-permute-start | bytes 73736 | tf_op jit(solution)/shard_map/ppermute | solution.py:424
  5.6 4.7 %collective-permute-start.5 = (f32[8,768]{1,0:T(8,128)S(1)}, f32[8,768]{1,0:T(8,128)S(1)}, u32[]{:S(2)}, u32[]{:S(2)}) collective-permute-start(f32[8,768]{1,0:T(8,128)S(1)} %get-tuple-element.13.refs_0_), channel_id=1, source_target_pairs={{0,24},{4,28},{8,16},{12,20},{16,8},{20,12},{24,0},{28,4},{1,25},{... | collective-permute-start | bytes 73736 | tf_op jit(solution)/shard_map/ppermute | solution.py:424
  5.6 4.9 %collective-permute-start = (f32[8,768]{1,0:T(8,128)S(1)}, f32[8,768]{1,0:T(8,128)S(1)}, u32[]{:S(2)}, u32[]{:S(2)}) collective-permute-start(f32[8,768]{1,0:T(8,128)S(1)} %get-tuple-element.13.refs_0_), channel_id=1, source_target_pairs={{0,4},{4,0},{8,12},{12,8},{16,20},{20,16},{24,28},{28,24},{1,5},{5... | collective-permute-start | bytes 73736 | tf_op jit(solution)/shard_map/ppermute | solution.py:424
  6.5 3.9 %collective-permute-start.2 = (f32[8,768]{1,0:T(8,128)S(1)}, f32[8,768]{1,0:T(8,128)S(1)}, u32[]{:S(2)}, u32[]{:S(2)}) collective-permute-start(f32[8,768]{1,0:T(8,128)S(1)} %collective-permute-done.1.refs_2_), channel_id=1, source_target_pairs={{0,4},{4,0},{8,12},{12,8},{16,20},{20,16},{24,28},{28,24},{1,5},{5... | collective-permute-start | bytes 73736 | tf_op jit(solution)/shard_map/ppermute | solution.py:424
  7.9 2.6 %collective-permute-start.4 = (f32[8,768]{1,0:T(8,128)S(1)}, f32[8,768]{1,0:T(8,128)S(1)}, u32[]{:S(2)}, u32[]{:S(2)}) collective-permute-start(f32[8,768]{1,0:T(8,128)S(1)} %collective-permute-done.3.refs_4_), channel_id=1, source_target_pairs={{0,4},{4,0},{8,12},{12,8},{16,20},{20,16},{24,28},{28,24},{1,5},{5... | collective-permute-start | bytes 73736 | tf_op jit(solution)/shard_map/ppermute | solution.py:424
  10.3 1.2 %collective-permute-start.6 = (f32[8,768]{1,0:T(8,128)S(1)}, f32[8,768]{1,0:T(8,128)S(1)}, u32[]{:S(2)}, u32[]{:S(2)}) collective-permute-start(f32[8,768]{1,0:T(8,128)S(1)} %collective-permute-done.5.refs_6_), channel_id=1, source_target_pairs={{0,4},{4,0},{8,12},{12,8},{16,20},{20,16},{24,28},{28,24},{1,5},{5... | collective-permute-start | bytes 73736 | tf_op jit(solution)/shard_map/ppermute | solution.py:424
  25.9 9.9 %collective-permute-start.7 = (bf16[64,256]{1,0:T(8,128)(2,1)S(1)}, bf16[64,256]{1,0:T(8,128)(2,1)S(1)}, u32[]{:S(2)}, u32[]{:S(2)}) collective-permute-start(bf16[64,256]{1,0:T(8,128)(2,1)S(1)} %get-tuple-element.22), channel_id=1, source_target_pairs={{0,1},{1,0},{2,3},{3,2},{4,5},{5,4},{6,7},{7,6},{8,9},{9,8},{10,11... | collective-permute-start | bytes 98312 | tf_op jit(solution)/shard_map/ppermute | solution.py:424
  31.3 5.2 %collective-permute-start.8 = (bf16[64,256]{1,0:T(8,128)(2,1)S(1)}, bf16[64,256]{1,0:T(8,128)(2,1)S(1)}, u32[]{:S(2)}, u32[]{:S(2)}) collective-permute-start(bf16[64,256]{1,0:T(8,128)(2,1)S(1)} %get-tuple-element.21), channel_id=1, source_target_pairs={{0,2},{1,3},{2,0},{3,1},{4,6},{5,7},{6,4},{7,5},{8,10},{9,11},{10,... | collective-permute-start | bytes 98312 | tf_op jit(solution)/shard_map/ppermute | solution.py:424
  31.7 5.7 %collective-permute-start.9 = (bf16[64,256]{1,0:T(8,128)(2,1)S(1)}, bf16[64,256]{1,0:T(8,128)(2,1)S(1)}, u32[]{:S(2)}, u32[]{:S(2)}) collective-permute-start(bf16[64,256]{1,0:T(8,128)(2,1)S(1)} %get-tuple-element.20), channel_id=1, source_target_pairs={{0,3},{1,2},{2,1},{3,0},{4,7},{5,6},{6,5},{7,4},{8,11},{9,10},{10,... | collective-permute-start | bytes 98312 | tf_op jit(solution)/shard_map/ppermute | solution.py:424
  37.4 5.3 %collective-permute-start.11 = (bf16[256,256]{1,0:T(8,128)(2,1)S(1)}, bf16[256,256]{1,0:T(8,128)(2,1)S(1)}, u32[]{:S(2)}, u32[]{:S(2)}) collective-permute-start(bf16[256,256]{1,0:T(8,128)(2,1)S(1)} %pad_maximum_fusion.refs_0_), channel_id=1, source_target_pairs={{0,8},{4,12},{8,0},{12,4},{16,24},{20,28},{24,16},{28,20},{1,9},{5... | collective-permute-start | bytes 393224 | tf_op jit(solution)/shard_map/ppermute | solution.py:424
  37.9 6.5 %collective-permute-start.12 = (bf16[256,256]{1,0:T(8,128)(2,1)S(1)}, bf16[256,256]{1,0:T(8,128)(2,1)S(1)}, u32[]{:S(2)}, u32[]{:S(2)}) collective-permute-start(bf16[256,256]{1,0:T(8,128)(2,1)S(1)} %pad_maximum_fusion.refs_0_), channel_id=1, source_target_pairs={{0,16},{4,20},{8,24},{12,28},{16,0},{20,4},{24,8},{28,12},{1,17},{... | collective-permute-start | bytes 393224 | tf_op jit(solution)/shard_map/ppermute | solution.py:424
  38.1 6.3 %collective-permute-start.13 = (bf16[256,256]{1,0:T(8,128)(2,1)S(1)}, bf16[256,256]{1,0:T(8,128)(2,1)S(1)}, u32[]{:S(2)}, u32[]{:S(2)}) collective-permute-start(bf16[256,256]{1,0:T(8,128)(2,1)S(1)} %pad_maximum_fusion.refs_0_), channel_id=1, source_target_pairs={{0,24},{4,28},{8,16},{12,20},{16,8},{20,12},{24,0},{28,4},{1,25},{... | collective-permute-start | bytes 393224 | tf_op jit(solution)/shard_map/ppermute | solution.py:424
  41.0 3.9 %collective-permute-start.10 = (bf16[256,256]{1,0:T(8,128)(2,1)S(1)}, bf16[256,256]{1,0:T(8,128)(2,1)S(1)}, u32[]{:S(2)}, u32[]{:S(2)}) collective-permute-start(bf16[256,256]{1,0:T(8,128)(2,1)S(1)} %pad_maximum_fusion.refs_0_), channel_id=1, source_target_pairs={{0,4},{4,0},{8,12},{12,8},{16,20},{20,16},{24,28},{28,24},{1,5},{5... | collective-permute-start | bytes 393224 | tf_op jit(solution)/shard_map/ppermute | solution.py:424
  42.8 2.8 %collective-permute-start.14 = (bf16[256,256]{1,0:T(8,128)(2,1)S(1)}, bf16[256,256]{1,0:T(8,128)(2,1)S(1)}, u32[]{:S(2)}, u32[]{:S(2)}) collective-permute-start(bf16[256,256]{1,0:T(8,128)(2,1)S(1)} %collective-permute-done.11.refs_1_), channel_id=1, source_target_pairs={{0,4},{4,0},{8,12},{12,8},{16,20},{20,16},{24,28},{28,24},{1,5},{5... | collective-permute-start | bytes 393224 | tf_op jit(solution)/shard_map/ppermute | solution.py:424
  44.4 1.3 %collective-permute-start.15 = (bf16[256,256]{1,0:T(8,128)(2,1)S(1)}, bf16[256,256]{1,0:T(8,128)(2,1)S(1)}, u32[]{:S(2)}, u32[]{:S(2)}) collective-permute-start(bf16[256,256]{1,0:T(8,128)(2,1)S(1)} %collective-permute-done.12.refs_2_), channel_id=1, source_target_pairs={{0,4},{4,0},{8,12},{12,8},{16,20},{20,16},{24,28},{28,24},{1,5},{5... | collective-permute-start | bytes 393224 | tf_op jit(solution)/shard_map/ppermute | solution.py:424
  44.4 1.5 %collective-permute-start.16 = (bf16[256,256]{1,0:T(8,128)(2,1)S(1)}, bf16[256,256]{1,0:T(8,128)(2,1)S(1)}, u32[]{:S(2)}, u32[]{:S(2)}) collective-permute-start(bf16[256,256]{1,0:T(8,128)(2,1)S(1)} %collective-permute-done.13.refs_3_), channel_id=1, source_target_pairs={{0,4},{4,0},{8,12},{12,8},{16,20},{20,16},{24,28},{28,24},{1,5},{5... | collective-permute-start | bytes 393224 | tf_op jit(solution)/shard_map/ppermute | solution.py:424
where the time goes:
time: 47.3 us; the launch traced here: 47.1 us
  Pallas kernels  19.2 us (41%)
  starting transfers between devices  17.1 us (36%)
  waiting for transfers between devices  9.64 us (20%)
  other arithmetic  0.93 us (2%)
    ppermute x17, starting transfers between devices, swap(): return lax.ppermute(x, axis, [(i, i ^ mask) for i in range(size)])  17.1 us
    pallas_call x1, Pallas kernels, echoes(): pl.pallas_call(functools.partial(echo_kernel, pieces, blocks, groups, gro...  14.3 us
    ppermute x17, waiting for transfers between devices, swap(): return lax.ppermute(x, axis, [(i, i ^ mask) for i in range(size)])  9.64 us
    pallas_call x1, Pallas kernels, transform_tables(): pl.pallas_call(functools.partial(transform_tables_kernel, facet_n, pulse_...  2 us
    pallas_call x3, Pallas kernels, transform(): pl.pallas_call(functools.partial(transform_kernel, places, total is not N...  1.85 us
    pallas_call x1, Pallas kernels, pack_facets(): pl.pallas_call(functools.partial(pack_kernel, groups, group_len), out_sha...  1.01 us
  transfers between devices with their start and end apart: 17, of which 9 were waited for; matrix products, arithmetic and copies ran while one was open for 2% of the time, Pallas kernels for 6%

commit v1 on v0

--- a/solution.py
+++ b/solution.py
@@ -14,7 +14,8 @@
 PBS = 32
 BINS = 512
 LANES = 128
-STEP = 4
+WIDE = 8
+NARROW = 4
 QUADS = 4
 
 
@@ -47,13 +48,13 @@
             left[m * 4 + which, c, plus] = sign
             left[m * 4 + which, c, minus] = (sign, -sign)[which % 2]
     right = np.zeros((16, 2, 2, 16))
-    for mp in range(2):
-        for m in range(2):
-            for low in range(2):
-                middle, off = 4 + 8 * (2 * mp + low), (1, 3)[m]
-                for which, (cs, plus, minus) in enumerate(((0, 1, 1), (0, -1, 1), (1, 1, 1), (1, 1, -1))):
-                    right[mp * 8 + m * 4 + which, low, cs, (middle + off - 1) // 2] = plus
-                    right[mp * 8 + m * 4 + which, low, cs, (middle - off - 1) // 2] = minus
+    for f16, ff, m, fn in np.ndindex(2, 2, 2, 2):
+        for low in range(2):
+            for e, d in ((1, 1), (1, -1), (-1, 1), (-1, -1)):
+                far, near = (4, 12)[low], (1, 3)[m]
+                sines = f16 + ff + fn
+                value = (e if ff else 1) * (d if fn else 1) * (-1) ** (sines // 2)
+                right[f16 * 8 + ff * 4 + m * 2 + fn, low, sines % 2, (15 + e * far + d * near) // 2] = value
     both = np.einsum("tca,ulsj->tulcsaj", left, right)
     out = np.zeros((8, 16, 2, 2, 4, 32))
     up, down = slice(16, 32), slice(15, None, -1)
@@ -61,7 +62,7 @@
     out[:, :, :, 0, :, down] = both[:, :, :, 0, 0] - both[:, :, :, 1, 1]
     out[:, :, :, 1, :, up] = both[:, :, :, 1, 0] - both[:, :, :, 0, 1]
     out[:, :, :, 1, :, down] = both[:, :, :, 1, 0] + both[:, :, :, 0, 1]
-    return out.reshape(8 * 32, 2 * 4 * 32) / 16.0
+    return out.reshape(8 * 32, 2 * 4 * 32) / 32.0
 
 
 def pack(low, high):
@@ -84,8 +85,6 @@
     a4, b4 = a2 * a2 - 2.0, a2 * b2
     a8, b8 = a4 * a4 - 2.0, a4 * b4
     a12, b12 = (a8 - 1.0) * a4, (a8 + 1.0) * b4
-    a20, b20 = a8 * a12 - a4, a8 * b12 - b4
-    a28, b28 = a8 * a20 - a12, a8 * b20 - b12
     a16, b16 = a8 * a8 - 2.0, a8 * b8
     a32, b32 = a16 * a16 - 2.0, a16 * b16
     a64, b64 = a32 * a32 - 2.0, a32 * b32
@@ -101,19 +100,26 @@
     q3r, q3i = a256 * q2r - q1r, a256 * q2i - q1i
     return (
         a32, b32, a96, b96, q0r, q0i, q1r, q1i, q2r, q2i, q3r, q3i,
-        c1, s1, c3, s3, a4, b4, a12, b12, a20, b20, a28, b28,
+        a16, b16, a4, b4, a12, b12, c1, s1, c3, s3,
     )
 
 
-def table_of(factors):
-    near, far = factors[:4], factors[4:]
-    near = [pack(value, value) for value in near]
+def left_table(factors):
+    near = [pack(value, value) for value in factors[:4]]
+    far = factors[4:]
     tiles = []
     for low in (0, 4):
         real, imag = pack(far[low], far[low + 2]), pack(far[low + 1], far[low + 3])
         for cosine, sine in (near[0:2], near[2:4]):
             tiles += [real * cosine, imag * sine, imag * cosine, real * sine]
     return jnp.concatenate(tiles, axis=0)
+
+
+def right_table(factors):
+    middle = [pack(value, value) for value in factors[:2]]
+    far = [pack(factors[2], factors[4]), pack(factors[3], factors[5])]
+    near = [pack(value, value) for value in factors[6:]]
+    return jnp.concatenate([(m * f) * n for m in middle for f in far for n in near], axis=0)
 
 
 def echo_kernel(
@@ -144,7 +150,7 @@
     antenna[:pulse_dev, :8] = flat.T
     antenna[pulse_dev:, :] = jnp.zeros((8, LANES), f32)
     marks_copy.wait()
-    most = pieces * blocks + 3 * STEP
+    most = pieces * blocks + 2 * WIDE
 
     def scan(piece, g, at):
         for j in range(blocks):
@@ -153,7 +159,7 @@
         return at
 
     def close(at):
-        for extra in range(3 * STEP):
+        for extra in range(2 * WIDE):
             rows_s[at + extra] = pieces * blocks * 8
 
     def station(g):
@@ -162,15 +168,15 @@
         return [jnp.broadcast_to(ant[:, i : i + 1], (8, LANES)) for i in range(3)]
 
     def turn(at, place):
-        for j in range(STEP):
+        for j in range(WIDE):
             row = rows_s[at + j]
             facet = [fac_ref[pl.ds(row + c, 8, stride=0), :] for c in range(3)]
             angles[j, 0], angles[j, 1] = block_angles(*facet, *place)
 
-    def read(at, j):
+    def read(at, slot, j):
         row = rows_s[at + j]
         weights = [fac_ref[pl.ds(row + c, 8, stride=0), :] for c in (3, 4)]
-        return angles[j, 0], angles[j, 1], *weights
+        return angles[slot + j, 0], angles[slot + j, 1], *weights
 
     same = (
         lax.broadcasted_iota(jnp.int32, (16, 256), 0) % 8
@@ -180,21 +186,33 @@
     def group(acc0, acc1, g, count):
         place = station(g)
         here, there = (g % 2) * most, ((g + 1) % 2) * most
-        steps = jnp.maximum(lax.div(count + (STEP - 1), STEP), 1)
-
-        def step(i, at):
-            for half, acc in ((0, acc0), (1, acc1)):
-                pair = [block_factors(*read(here + i * STEP, 2 * half + j)) for j in range(2)]
-                right = jnp.concatenate([table_of(p[12:]) for p in pair], axis=1)
-                left = jnp.concatenate([table_of(p[:12]) for p in pair], axis=1)
-                pltpu.matmul_push_rhs(right, staging_register=0, mxu_index=half, transpose=True)
-                pltpu.matmul_acc_lhs(acc, left, load_staged_rhs=0)
-            turn(here + (i + 1) * STEP, place)
-            return scan(jnp.minimum(i, pieces), g + 1, at)
-
-        at = lax.fori_loop(0, steps, step, there)
+        wide = lax.div(count, WIDE)
+        narrow = lax.div(count - wide * WIDE + (NARROW - 1), NARROW)
+        narrow = jnp.maximum(narrow, 1 - wide)
+
+        def multiply(at, slot, blocks_here):
+            for half in range(blocks_here // 2):
+                pair = [block_factors(*read(at, slot, 2 * half + j)) for j in range(2)]
+                right = jnp.concatenate([right_table(p[12:]) for p in pair], axis=1)
+                left = jnp.concatenate([left_table(p[:12]) for p in pair], axis=1)
+                unit, register = half % 2, half // 2
+                pltpu.matmul_push_rhs(right, staging_register=register, mxu_index=unit, transpose=True)
+                pltpu.matmul_acc_lhs((acc0, acc1)[unit], left, load_staged_rhs=register)
+
+        def wide_step(i, at):
+            multiply(here + i * WIDE, 0, WIDE)
+            turn(here + (i + 1) * WIDE, place)
+            at = scan(jnp.minimum(2 * i, pieces), g + 1, at)
+            return scan(jnp.minimum(2 * i + 1, pieces), g + 1, at)
+
+        def narrow_step(i, at):
+            multiply(here + wide * WIDE + i * NARROW, i * NARROW, NARROW)
+            return scan(jnp.minimum(2 * wide + i, pieces), g + 1, at)
+
+        at = lax.fori_loop(0, wide, wide_step, there)
+        at = lax.fori_loop(0, narrow, narrow_step, at)
         at = lax.fori_loop(
-            jnp.minimum(steps, pieces), pieces, lambda piece, n: scan(piece, g + 1, n), at
+            jnp.minimum(2 * wide + narrow, pieces), pieces, lambda piece, n: scan(piece, g + 1, n), at
         )
         close(at)
         turn(there, station(g + 1))
@@ -233,7 +251,7 @@
 
 def echoes(buildings, platform, fold, facets, blocks, groups, group_len):
     pieces = len(facets)
-    most = pieces * blocks + 3 * STEP
+    most = pieces * blocks + 2 * WIDE
     pulse_dev = platform.shape[1]
     vmem = pl.BlockSpec(memory_space=pltpu.VMEM)
     return pl.pallas_call(
@@ -245,9 +263,9 @@
             pltpu.VMEM(((pieces * blocks + 1) * 8, LANES), f32),
             pltpu.VMEM((pieces + 8, LANES), jnp.int32),
             pltpu.SMEM((pieces + 8, LANES), jnp.int32),
-            pltpu.SMEM((2 * most + 3 * STEP,), jnp.int32),
+            pltpu.SMEM((2 * most + 2 * WIDE,), jnp.int32),
             pltpu.VMEM((pulse_dev + 8, LANES), f32),
-            pltpu.VMEM((STEP, 2, 8, LANES), f32),
+            pltpu.VMEM((WIDE, 2, 8, LANES), f32),
             pltpu.VMEM((2, groups * 16, 2048), bf16),
             pltpu.SemaphoreType.DMA,
         ],

time: 47.3 us -> 45.7 us (0.966)
  Pallas kernels: 19.2 us -> 17.5 us
    pallas_call x1, Pallas kernels: 14.3 us -> 12.7 us  [echoes(): pl.pallas_call(functools.partial(echo_kernel, pieces, blocks, groups, gro...]
where the time goes in v1:
time: 45.7 us; the launch traced here: 45.5 us
  Pallas kernels  17.5 us (38%)
  starting transfers between devices  16.8 us (37%)
  waiting for transfers between devices  9.92 us (22%)
  other arithmetic  0.93 us (2%)
    ppermute x17, starting transfers between devices, swap(): return lax.ppermute(x, axis, [(i, i ^ mask) for i in range(size)])  16.8 us
    pallas_call x1, Pallas kernels, echoes(): pl.pallas_call(functools.partial(echo_kernel, pieces, blocks, groups, gro...  12.7 us
    ppermute x17, waiting for transfers between devices, swap(): return lax.ppermute(x, axis, [(i, i ^ mask) for i in range(size)])  9.92 us
    pallas_call x1, Pallas kernels, transform_tables(): pl.pallas_call(functools.partial(transform_tables_kernel, facet_n, pulse_...  2 us
    pallas_call x3, Pallas kernels, transform(): pl.pallas_call(functools.partial(transform_kernel, places, total is not N...  1.85 us
    pallas_call x1, Pallas kernels, pack_facets(): pl.pallas_call(functools.partial(pack_kernel, groups, group_len), out_sha...  1.01 us
    mul x1, other arithmetic, body(): jnp.broadcast_to(jnp.asarray(fold_matrix(), bf16)[:, None, :], (256, 8, 2...  0.92 us
  transfers between devices with their start and end apart: 17, of which 9 were waited for; matrix products, arithmetic and copies ran while one was open for 2% of the time, Pallas kernels for 6%

profile of v1, /device:TPU:0, one launch (start us, length us, event | category | flops | bytes accessed | tf_op | source)
XLA Modules:
  0.0 45.5 jit_solution(17893783227942451363)
XLA Ops:
  0.0 1.0 %pack_facets.1 = (f32[8,768]{1,0:T(8,128)S(1)}, f32[3,512]{1,0:T(4,128)S(1)}) custom-call(s32[6]{0:T(128)} %ids_hbm.1, f32[3,768]{1,0:T(4,128)} %positions_hbm.1, f32[2,768]{1,0:T(2,128)} %reflectivity_hbm.1, s32[12,16]{1,0:T(8,128)} %visible_hbm.1, f32[3,512]{1,0:T(4,128)} %platform_hbm.1), custom_call_target="tpu_custom_call" | custom-call | tf_op jit(solution)/shard_map/pack_facets/pallas_call | solution.py:318
  1.0 3.0 %collective-permute-start.1 = (f32[8,768]{1,0:T(8,128)S(1)}, f32[8,768]{1,0:T(8,128)S(1)}, u32[]{:S(2)}, u32[]{:S(2)}) collective-permute-start(f32[8,768]{1,0:T(8,128)S(1)} %get-tuple-element.13.refs_0_), channel_id=1, source_target_pairs={{0,8},{4,12},{8,0},{12,4},{16,24},{20,28},{24,16},{28,20},{1,9},{5... | collective-permute-start | bytes 73736 | tf_op jit(solution)/shard_map/ppermute | solution.py:442
  4.1 1.5 %collective-permute-start.3 = (f32[8,768]{1,0:T(8,128)S(1)}, f32[8,768]{1,0:T(8,128)S(1)}, u32[]{:S(2)}, u32[]{:S(2)}) collective-permute-start(f32[8,768]{1,0:T(8,128)S(1)} %get-tuple-element.13.refs_0_), channel_id=1, source_target_pairs={{0,16},{4,20},{8,24},{12,28},{16,0},{20,4},{24,8},{28,12},{1,17},{... | collective-permute-start | bytes 73736 | tf_op jit(solution)/shard_map/ppermute | solution.py:442
  5.6 0.0 collective-permute-start.5
  5.6 0.0 collective-permute-start
  5.6 0.9 %broadcast_multiply_fusion = bf16[256,256]{1,0:T(8,128)(2,1)S(1)} fusion(bf16[256,256]{1,0:T(8,128)(2,1)} %constant.30.clone, bf16[]{:T(256)S(6)} %convert_element_type.3), kind=kLoop, calls=%fused_computation.2 | loop fusion | flops 65536 | bytes 262146 | tf_op jit(solution)/shard_map/mul | solution.py:475
  6.5 0.0 collective-permute-done.1.refs_2_
  6.5 0.6 %collective-permute-start.2 = (f32[8,768]{1,0:T(8,128)S(1)}, f32[8,768]{1,0:T(8,128)S(1)}, u32[]{:S(2)}, u32[]{:S(2)}) collective-permute-start(f32[8,768]{1,0:T(8,128)S(1)} %collective-permute-done.1.refs_2_), channel_id=1, source_target_pairs={{0,4},{4,0},{8,12},{12,8},{16,20},{20,16},{24,28},{28,24},{1,5},{5... | collective-permute-start | bytes 73736 | tf_op jit(solution)/shard_map/ppermute | solution.py:442
  7.1 0.8 %collective-permute-done.3.refs_4_ = f32[8,768]{1,0:T(8,128)S(1)} collective-permute-done((f32[8,768]{1,0:T(8,128)S(1)}, f32[8,768]{1,0:T(8,128)S(1)}, u32[]{:S(2)}, u32[]{:S(2)}) %collective-permute-start.3) | collective-permute-done | bytes 24608 | tf_op jit(solution)/shard_map/ppermute | solution.py:442
  7.9 0.0 collective-permute-start.4
  7.9 2.4 %collective-permute-done.5.refs_6_ = f32[8,768]{1,0:T(8,128)S(1)} collective-permute-done((f32[8,768]{1,0:T(8,128)S(1)}, f32[8,768]{1,0:T(8,128)S(1)}, u32[]{:S(2)}, u32[]{:S(2)}) %collective-permute-start.5) | collective-permute-done | bytes 24608 | tf_op jit(solution)/shard_map/ppermute | solution.py:442
  10.3 0.0 collective-permute-start.6
  10.3 0.1 broadcast_bitcast_fusion.fold
  10.5 0.0 collective-permute-done.refs_1_
  10.5 0.0 collective-permute-done.2.refs_3_
  10.5 0.0 collective-permute-done.4.refs_5_
  10.5 1.0 %collective-permute-done.6.refs_7_ = f32[8,768]{1,0:T(8,128)S(1)} collective-permute-done((f32[8,768]{1,0:T(8,128)S(1)}, f32[8,768]{1,0:T(8,128)S(1)}, u32[]{:S(2)}, u32[]{:S(2)}) %collective-permute-start.6) | collective-permute-done | bytes 24608 | tf_op jit(solution)/shard_map/ppermute | solution.py:442
  11.5 12.7 %echoes.1.after_ref = bf16[4,64,256]{2,1,0:T(8,128)(2,1)S(1)} custom-call(f32[3,512]{1,0:T(4,128)S(1)} %get-tuple-element.12.platform_ref, bf16[2048,256]{1,0:T(8,128)(2,1)S(1)} %broadcast_bitcast_fusion.fold, f32[8,768]{1,0:T(8,128)S(1)} %get-tuple-element.13.refs_0_, f32[8,768]{1,0:T(8,128)S(1)} %collective-permute-done.refs_1_, ...), custom_call_target="tpu_custom_call" | custom-call | tf_op jit(solution)/shard_map/echoes/pallas_call | solution.py:257
  24.2 5.1 %collective-permute-start.7 = (bf16[64,256]{1,0:T(8,128)(2,1)S(1)}, bf16[64,256]{1,0:T(8,128)(2,1)S(1)}, u32[]{:S(2)}, u32[]{:S(2)}) collective-permute-start(bf16[64,256]{1,0:T(8,128)(2,1)S(1)} %get-tuple-element.22), channel_id=1, source_target_pairs={{0,1},{1,0},{2,3},{3,2},{4,5},{5,4},{6,7},{7,6},{8,9},{9,8},{10,11... | collective-permute-start | bytes 98312 | tf_op jit(solution)/shard_map/ppermute | solution.py:442
  29.4 0.7 %collective-permute-start.8 = (bf16[64,256]{1,0:T(8,128)(2,1)S(1)}, bf16[64,256]{1,0:T(8,128)(2,1)S(1)}, u32[]{:S(2)}, u32[]{:S(2)}) collective-permute-start(bf16[64,256]{1,0:T(8,128)(2,1)S(1)} %get-tuple-element.21), channel_id=1, source_target_pairs={{0,2},{1,3},{2,0},{3,1},{4,6},{5,7},{6,4},{7,5},{8,10},{9,11},{10,... | collective-permute-start | bytes 98312 | tf_op jit(solution)/shard_map/ppermute | solution.py:442
  30.1 1.7 %collective-permute-start.9 = (bf16[64,256]{1,0:T(8,128)(2,1)S(1)}, bf16[64,256]{1,0:T(8,128)(2,1)S(1)}, u32[]{:S(2)}, u32[]{:S(2)}) collective-permute-start(bf16[64,256]{1,0:T(8,128)(2,1)S(1)} %get-tuple-element.20), channel_id=1, source_target_pairs={{0,3},{1,2},{2,1},{3,0},{4,7},{5,6},{6,5},{7,4},{8,11},{9,10},{10,... | collective-permute-start | bytes 98312 | tf_op jit(solution)/shard_map/ppermute | solution.py:442
  31.8 2.0 %transform_tables.1 = (bf16[512,2048]{1,0:T(8,128)(2,1)S(1)}, f32[2,256,128]{2,1,0:T(8,128)S(1)}) custom-call(bf16[4,64,256]{2,1,0:T(8,128)(2,1)S(1)} %echoes.1.after_ref), custom_call_target="tpu_custom_call" | custom-call | tf_op jit(solution)/shard_map/transform_tables/pallas_call | solution.py:388
  33.8 0.0 collective-permute-done.7
  33.8 0.8 %collective-permute-done.8 = bf16[64,256]{1,0:T(8,128)(2,1)S(1)} collective-permute-done((bf16[64,256]{1,0:T(8,128)(2,1)S(1)}, bf16[64,256]{1,0:T(8,128)(2,1)S(1)}, u32[]{:S(2)}, u32[]{:S(2)}) %collective-permute-start.8) | collective-permute-done | bytes 32800 | tf_op jit(solution)/shard_map/ppermute | solution.py:442
  34.7 1.1 %collective-permute-done.9 = bf16[64,256]{1,0:T(8,128)(2,1)S(1)} collective-permute-done((bf16[64,256]{1,0:T(8,128)(2,1)S(1)}, bf16[64,256]{1,0:T(8,128)(2,1)S(1)}, u32[]{:S(2)}, u32[]{:S(2)}) %collective-permute-start.9) | collective-permute-done | bytes 32800 | tf_op jit(solution)/shard_map/ppermute | solution.py:442
  35.8 0.6 %collective-permute-start.11 = (bf16[256,256]{1,0:T(8,128)(2,1)S(1)}, bf16[256,256]{1,0:T(8,128)(2,1)S(1)}, u32[]{:S(2)}, u32[]{:S(2)}) collective-permute-start(bf16[256,256]{1,0:T(8,128)(2,1)S(1)} %pad_maximum_fusion.refs_0_), channel_id=1, source_target_pairs={{0,8},{4,12},{8,0},{12,4},{16,24},{20,28},{24,16},{28,20},{1,9},{5... | collective-permute-start | bytes 393224 | tf_op jit(solution)/shard_map/ppermute | solution.py:442
  36.4 0.3 collective-permute-start.12
  36.6 2.7 %collective-permute-start.13 = (bf16[256,256]{1,0:T(8,128)(2,1)S(1)}, bf16[256,256]{1,0:T(8,128)(2,1)S(1)}, u32[]{:S(2)}, u32[]{:S(2)}) collective-permute-start(bf16[256,256]{1,0:T(8,128)(2,1)S(1)} %pad_maximum_fusion.refs_0_), channel_id=1, source_target_pairs={{0,24},{4,28},{8,16},{12,20},{16,8},{20,12},{24,0},{28,4},{1,25},{... | collective-permute-start | bytes 393224 | tf_op jit(solution)/shard_map/ppermute | solution.py:442
  39.3 0.0 collective-permute-start.10
  39.3 1.8 %collective-permute-done.11.refs_1_ = bf16[256,256]{1,0:T(8,128)(2,1)S(1)} collective-permute-done((bf16[256,256]{1,0:T(8,128)(2,1)S(1)}, bf16[256,256]{1,0:T(8,128)(2,1)S(1)}, u32[]{:S(2)}, u32[]{:S(2)}) %collective-permute-start.11) | collective-permute-done | bytes 131104 | tf_op jit(solution)/shard_map/ppermute | solution.py:442
  41.1 0.0 collective-permute-start.14
  41.1 1.6 %collective-permute-done.12.refs_2_ = bf16[256,256]{1,0:T(8,128)(2,1)S(1)} collective-permute-done((bf16[256,256]{1,0:T(8,128)(2,1)S(1)}, bf16[256,256]{1,0:T(8,128)(2,1)S(1)}, u32[]{:S(2)}, u32[]{:S(2)}) %collective-permute-start.12) | collective-permute-done | bytes 131104 | tf_op jit(solution)/shard_map/ppermute | solution.py:442
  42.8 0.0 collective-permute-start.15
  42.8 0.0 collective-permute-done.13.refs_3_
  42.8 0.5 %collective-permute-start.16 = (bf16[256,256]{1,0:T(8,128)(2,1)S(1)}, bf16[256,256]{1,0:T(8,128)(2,1)S(1)}, u32[]{:S(2)}, u32[]{:S(2)}) collective-permute-start(bf16[256,256]{1,0:T(8,128)(2,1)S(1)} %collective-permute-done.13.refs_3_), channel_id=1, source_target_pairs={{0,4},{4,0},{8,12},{12,8},{16,20},{20,16},{24,28},{28,24},{1,5},{5... | collective-permute-start | bytes 393224 | tf_op jit(solution)/shard_map/ppermute | solution.py:442
  43.3 0.0 collective-permute-done.10.refs_1_
  43.3 0.3 transform.3.refs_0_
  43.6 0.4 transform.4.refs_0_
  44.0 0.0 collective-permute-done.14.refs_1_
  44.0 0.1 collective-permute-done.15.refs_2_
  44.1 0.2 collective-permute-done.16.refs_3_
  44.3 1.2 %transform.5 = f32[2,128,256]{2,1,0:T(8,128)} custom-call(bf16[512,2048]{1,0:T(8,128)(2,1)S(1)} %get-tuple-element.16.w_ref, f32[512,256]{1,0:T(8,128)S(1)} %transform.4.refs_0_, bf16[256,256]{1,0:T(8,128)(2,1)S(1)} %collective-permute-done.14.refs_1_, bf16[256,256]{1,0:T(8,128)(2,1)S(1)} %collective-permute-done.15.refs_2_, ...), custom_call_target="tpu_custom_call" | custom-call | tf_op jit(solution)/shard_map/transform/pallas_call | solution.py:431
  (2 shorter events, 0.0 us)
Async XLA Ops:
  1.0 5.5 %collective-permute-start.1 = (f32[8,768]{1,0:T(8,128)S(1)}, f32[8,768]{1,0:T(8,128)S(1)}, u32[]{:S(2)}, u32[]{:S(2)}) collective-permute-start(f32[8,768]{1,0:T(8,128)S(1)} %get-tuple-element.13.refs_0_), channel_id=1, source_target_pairs={{0,8},{4,12},{8,0},{12,4},{16,24},{20,28},{24,16},{28,20},{1,9},{5... | collective-permute-start | bytes 73736 | tf_op jit(solution)/shard_map/ppermute | solution.py:442
  4.1 3.8 %collective-permute-start.3 = (f32[8,768]{1,0:T(8,128)S(1)}, f32[8,768]{1,0:T(8,128)S(1)}, u32[]{:S(2)}, u32[]{:S(2)}) collective-permute-start(f32[8,768]{1,0:T(8,128)S(1)} %get-tuple-element.13.refs_0_), channel_id=1, source_target_pairs={{0,16},{4,20},{8,24},{12,28},{16,0},{20,4},{24,8},{28,12},{1,17},{... | collective-permute-start | bytes 73736 | tf_op jit(solution)/shard_map/ppermute | solution.py:442
  5.6 4.7 %collective-permute-start.5 = (f32[8,768]{1,0:T(8,128)S(1)}, f32[8,768]{1,0:T(8,128)S(1)}, u32[]{:S(2)}, u32[]{:S(2)}) collective-permute-start(f32[8,768]{1,0:T(8,128)S(1)} %get-tuple-element.13.refs_0_), channel_id=1, source_target_pairs={{0,24},{4,28},{8,16},{12,20},{16,8},{20,12},{24,0},{28,4},{1,25},{... | collective-permute-start | bytes 73736 | tf_op jit(solution)/shard_map/ppermute | solution.py:442
  5.6 4.9 %collective-permute-start = (f32[8,768]{1,0:T(8,128)S(1)}, f32[8,768]{1,0:T(8,128)S(1)}, u32[]{:S(2)}, u32[]{:S(2)}) collective-permute-start(f32[8,768]{1,0:T(8,128)S(1)} %get-tuple-element.13.refs_0_), channel_id=1, source_target_pairs={{0,4},{4,0},{8,12},{12,8},{16,20},{20,16},{24,28},{28,24},{1,5},{5... | collective-permute-start | bytes 73736 | tf_op jit(solution)/shard_map/ppermute | solution.py:442
  6.5 3.9 %collective-permute-start.2 = (f32[8,768]{1,0:T(8,128)S(1)}, f32[8,768]{1,0:T(8,128)S(1)}, u32[]{:S(2)}, u32[]{:S(2)}) collective-permute-start(f32[8,768]{1,0:T(8,128)S(1)} %collective-permute-done.1.refs_2_), channel_id=1, source_target_pairs={{0,4},{4,0},{8,12},{12,8},{16,20},{20,16},{24,28},{28,24},{1,5},{5... | collective-permute-start | bytes 73736 | tf_op jit(solution)/shard_map/ppermute | solution.py:442
  7.9 2.6 %collective-permute-start.4 = (f32[8,768]{1,0:T(8,128)S(1)}, f32[8,768]{1,0:T(8,128)S(1)}, u32[]{:S(2)}, u32[]{:S(2)}) collective-permute-start(f32[8,768]{1,0:T(8,128)S(1)} %collective-permute-done.3.refs_4_), channel_id=1, source_target_pairs={{0,4},{4,0},{8,12},{12,8},{16,20},{20,16},{24,28},{28,24},{1,5},{5... | collective-permute-start | bytes 73736 | tf_op jit(solution)/shard_map/ppermute | solution.py:442
  10.3 1.2 %collective-permute-start.6 = (f32[8,768]{1,0:T(8,128)S(1)}, f32[8,768]{1,0:T(8,128)S(1)}, u32[]{:S(2)}, u32[]{:S(2)}) collective-permute-start(f32[8,768]{1,0:T(8,128)S(1)} %collective-permute-done.5.refs_6_), channel_id=1, source_target_pairs={{0,4},{4,0},{8,12},{12,8},{16,20},{20,16},{24,28},{28,24},{1,5},{5... | collective-permute-start | bytes 73736 | tf_op jit(solution)/shard_map/ppermute | solution.py:442
  24.2 9.6 %collective-permute-start.7 = (bf16[64,256]{1,0:T(8,128)(2,1)S(1)}, bf16[64,256]{1,0:T(8,128)(2,1)S(1)}, u32[]{:S(2)}, u32[]{:S(2)}) collective-permute-start(bf16[64,256]{1,0:T(8,128)(2,1)S(1)} %get-tuple-element.22), channel_id=1, source_target_pairs={{0,1},{1,0},{2,3},{3,2},{4,5},{5,4},{6,7},{7,6},{8,9},{9,8},{10,11... | collective-permute-start | bytes 98312 | tf_op jit(solution)/shard_map/ppermute | solution.py:442
  29.4 5.3 %collective-permute-start.8 = (bf16[64,256]{1,0:T(8,128)(2,1)S(1)}, bf16[64,256]{1,0:T(8,128)(2,1)S(1)}, u32[]{:S(2)}, u32[]{:S(2)}) collective-permute-start(bf16[64,256]{1,0:T(8,128)(2,1)S(1)} %get-tuple-element.21), channel_id=1, source_target_pairs={{0,2},{1,3},{2,0},{3,1},{4,6},{5,7},{6,4},{7,5},{8,10},{9,11},{10,... | collective-permute-start | bytes 98312 | tf_op jit(solution)/shard_map/ppermute | solution.py:442
  30.1 5.7 %collective-permute-start.9 = (bf16[64,256]{1,0:T(8,128)(2,1)S(1)}, bf16[64,256]{1,0:T(8,128)(2,1)S(1)}, u32[]{:S(2)}, u32[]{:S(2)}) collective-permute-start(bf16[64,256]{1,0:T(8,128)(2,1)S(1)} %get-tuple-element.20), channel_id=1, source_target_pairs={{0,3},{1,2},{2,1},{3,0},{4,7},{5,6},{6,5},{7,4},{8,11},{9,10},{10,... | collective-permute-start | bytes 98312 | tf_op jit(solution)/shard_map/ppermute | solution.py:442
  35.8 5.3 %collective-permute-start.11 = (bf16[256,256]{1,0:T(8,128)(2,1)S(1)}, bf16[256,256]{1,0:T(8,128)(2,1)S(1)}, u32[]{:S(2)}, u32[]{:S(2)}) collective-permute-start(bf16[256,256]{1,0:T(8,128)(2,1)S(1)} %pad_maximum_fusion.refs_0_), channel_id=1, source_target_pairs={{0,8},{4,12},{8,0},{12,4},{16,24},{20,28},{24,16},{28,20},{1,9},{5... | collective-permute-start | bytes 393224 | tf_op jit(solution)/shard_map/ppermute | solution.py:442
  36.4 6.4 %collective-permute-start.12 = (bf16[256,256]{1,0:T(8,128)(2,1)S(1)}, bf16[256,256]{1,0:T(8,128)(2,1)S(1)}, u32[]{:S(2)}, u32[]{:S(2)}) collective-permute-start(bf16[256,256]{1,0:T(8,128)(2,1)S(1)} %pad_maximum_fusion.refs_0_), channel_id=1, source_target_pairs={{0,16},{4,20},{8,24},{12,28},{16,0},{20,4},{24,8},{28,12},{1,17},{... | collective-permute-start | bytes 393224 | tf_op jit(solution)/shard_map/ppermute | solution.py:442
  36.6 6.1 %collective-permute-start.13 = (bf16[256,256]{1,0:T(8,128)(2,1)S(1)}, bf16[256,256]{1,0:T(8,128)(2,1)S(1)}, u32[]{:S(2)}, u32[]{:S(2)}) collective-permute-start(bf16[256,256]{1,0:T(8,128)(2,1)S(1)} %pad_maximum_fusion.refs_0_), channel_id=1, source_target_pairs={{0,24},{4,28},{8,16},{12,20},{16,8},{20,12},{24,0},{28,4},{1,25},{... | collective-permute-start | bytes 393224 | tf_op jit(solution)/shard_map/ppermute | solution.py:442
  39.3 3.9 %collective-permute-start.10 = (bf16[256,256]{1,0:T(8,128)(2,1)S(1)}, bf16[256,256]{1,0:T(8,128)(2,1)S(1)}, u32[]{:S(2)}, u32[]{:S(2)}) collective-permute-start(bf16[256,256]{1,0:T(8,128)(2,1)S(1)} %pad_maximum_fusion.refs_0_), channel_id=1, source_target_pairs={{0,4},{4,0},{8,12},{12,8},{16,20},{20,16},{24,28},{28,24},{1,5},{5... | collective-permute-start | bytes 393224 | tf_op jit(solution)/shard_map/ppermute | solution.py:442
  41.1 2.8 %collective-permute-start.14 = (bf16[256,256]{1,0:T(8,128)(2,1)S(1)}, bf16[256,256]{1,0:T(8,128)(2,1)S(1)}, u32[]{:S(2)}, u32[]{:S(2)}) collective-permute-start(bf16[256,256]{1,0:T(8,128)(2,1)S(1)} %collective-permute-done.11.refs_1_), channel_id=1, source_target_pairs={{0,4},{4,0},{8,12},{12,8},{16,20},{20,16},{24,28},{28,24},{1,5},{5... | collective-permute-start | bytes 393224 | tf_op jit(solution)/shard_map/ppermute | solution.py:442
  42.8 1.3 %collective-permute-start.15 = (bf16[256,256]{1,0:T(8,128)(2,1)S(1)}, bf16[256,256]{1,0:T(8,128)(2,1)S(1)}, u32[]{:S(2)}, u32[]{:S(2)}) collective-permute-start(bf16[256,256]{1,0:T(8,128)(2,1)S(1)} %collective-permute-done.12.refs_2_), channel_id=1, source_target_pairs={{0,4},{4,0},{8,12},{12,8},{16,20},{20,16},{24,28},{28,24},{1,5},{5... | collective-permute-start | bytes 393224 | tf_op jit(solution)/shard_map/ppermute | solution.py:442
  42.8 1.5 %collective-permute-start.16 = (bf16[256,256]{1,0:T(8,128)(2,1)S(1)}, bf16[256,256]{1,0:T(8,128)(2,1)S(1)}, u32[]{:S(2)}, u32[]{:S(2)}) collective-permute-start(bf16[256,256]{1,0:T(8,128)(2,1)S(1)} %collective-permute-done.13.refs_3_), channel_id=1, source_target_pairs={{0,4},{4,0},{8,12},{12,8},{16,20},{20,16},{24,28},{28,24},{1,5},{5... | collective-permute-start | bytes 393224 | tf_op jit(solution)/shard_map/ppermute | solution.py:442

commit v2 on v1

--- a/solution.py
+++ b/solution.py
@@ -63,6 +63,10 @@
     out[:, :, :, 1, :, up] = both[:, :, :, 1, 0] - both[:, :, :, 0, 1]
     out[:, :, :, 1, :, down] = both[:, :, :, 1, 0] + both[:, :, :, 0, 1]
     return out.reshape(8 * 32, 2 * 4 * 32) / 32.0
+
+
+def piece_rows(blocks):
+    return -(-(5 * blocks + 2) // 8) * 8
 
 
 def pack(low, high):
@@ -130,16 +134,17 @@
     out_ref, fac_ref, marks_v, marks_s, rows_s, antenna, angles, products, sem = refs[pieces:]
     mine = lax.axis_index("facet")
     in_turns = 1.0 / (16.0 * math.pi)
-    scale = jnp.where(lax.broadcasted_iota(jnp.int32, (8, LANES), 0) < 3, in_turns, 1.0)
+    rows = piece_rows(blocks)
+    scale = jnp.where(
+        lax.broadcasted_iota(jnp.int32, (rows, LANES), 0) < 3 * blocks, in_turns, 1.0
+    )
     for piece, ref in enumerate(piece_refs):
-        for j in range(blocks):
-            at = (piece * blocks + j) * 8
-            fac_ref[at : at + 8, :] = ref[:, j * LANES : j * LANES + LANES] * scale
-    fac_ref[pieces * blocks * 8 :, :] = jnp.zeros((8, LANES), f32)
-    ids = jnp.concatenate([ref[5:6, :LANES] for ref in piece_refs], axis=0)
+        fac_ref[piece * rows : piece * rows + rows, :] = ref[...] * scale
+    fac_ref[pieces * rows :, :] = jnp.zeros((rows, LANES), f32)
+    ids = jnp.concatenate([ref[5 * blocks : 5 * blocks + 1, :] for ref in piece_refs], axis=0)
     marks = jnp.zeros(ids.shape, jnp.int32)
     for b in range(buildings):
-        marks = jnp.where(ids == float(b), piece_refs[0][6:7, b : b + 1].astype(jnp.int32), marks)
+        marks = jnp.where(ids == float(b), piece_refs[0][5 * blocks + 1 : 5 * blocks + 2, b : b + 1].astype(jnp.int32), marks)
     marks_v[:pieces, :] = marks
     marks_v[pieces:, :] = jnp.zeros((8, LANES), jnp.int32)
     marks_copy = pltpu.make_async_copy(marks_v, marks_s, sem)
@@ -154,13 +159,13 @@
 
     def scan(piece, g, at):
         for j in range(blocks):
-            rows_s[at] = (piece * blocks + j) * 8
+            rows_s[at] = piece * rows + j
             at = at + (lax.shift_right_logical(marks_s[piece, j], g) & 1)
         return at
 
     def close(at):
         for extra in range(2 * WIDE):
-            rows_s[at + extra] = pieces * blocks * 8
+            rows_s[at + extra] = pieces * rows
 
     def station(g):
         g = jnp.minimum(g, groups - 1)
@@ -170,12 +175,12 @@
     def turn(at, place):
         for j in range(WIDE):
             row = rows_s[at + j]
-            facet = [fac_ref[pl.ds(row + c, 8, stride=0), :] for c in range(3)]
+            facet = [fac_ref[pl.ds(row + blocks * c, 8, stride=0), :] for c in range(3)]
             angles[j, 0], angles[j, 1] = block_angles(*facet, *place)
 
     def read(at, slot, j):
         row = rows_s[at + j]
-        weights = [fac_ref[pl.ds(row + c, 8, stride=0), :] for c in (3, 4)]
+        weights = [fac_ref[pl.ds(row + blocks * c, 8, stride=0), :] for c in (3, 4)]
         return angles[slot + j, 0], angles[slot + j, 1], *weights
 
     same = (
@@ -260,7 +265,7 @@
         in_specs=[vmem] * (2 + pieces),
         out_specs=vmem,
         scratch_shapes=[
-            pltpu.VMEM(((pieces * blocks + 1) * 8, LANES), f32),
+            pltpu.VMEM(((pieces + 1) * piece_rows(blocks), LANES), f32),
             pltpu.VMEM((pieces + 8, LANES), jnp.int32),
             pltpu.SMEM((pieces + 8, LANES), jnp.int32),
             pltpu.SMEM((2 * most + 2 * WIDE,), jnp.int32),
@@ -303,10 +308,17 @@
         words = jnp.where(lane == b, word, words)
     for copy in copies[2:]:
         copy.wait()
-    out_ref[0:3, :] = positions[...]
-    out_ref[3:5, :] = reflectivity[...]
-    out_ref[5:8, :LANES] = jnp.concatenate([row, words.astype(f32), jnp.zeros_like(row)], axis=0)
-    out_ref[5:8, LANES:] = jnp.zeros((3, out_ref.shape[1] - LANES), f32)
+    blocks = ids.shape[0]
+    for j in range(blocks):
+        lanes = slice(j * LANES, j * LANES + LANES)
+        for c in range(3):
+            out_ref[c * blocks + j : c * blocks + j + 1, :] = positions[c : c + 1, lanes]
+        for c in range(2):
+            at = (3 + c) * blocks + j
+            out_ref[at : at + 1, :] = reflectivity[c : c + 1, lanes]
+    left = out_ref.shape[0] - 5 * blocks
+    last = [row, words.astype(f32)] + [jnp.zeros_like(row)] * (left - 2)
+    out_ref[5 * blocks :, :] = jnp.concatenate(last, axis=0)
 
 
 def in_hbm(x):
@@ -318,7 +330,7 @@
     return pl.pallas_call(
         functools.partial(pack_kernel, groups, group_len),
         out_shape=(
-            jax.ShapeDtypeStruct((8, positions.shape[1]), f32),
+            jax.ShapeDtypeStruct((piece_rows(ids.shape[0]), LANES), f32),
             jax.ShapeDtypeStruct(platform.shape, f32),
         ),
         in_specs=[pl.BlockSpec(memory_space=pltpu.HBM)] * 5,
@@ -336,8 +348,7 @@
 
 
 def transform_tables_kernel(
-    facet_n, pulse_n, order, share, group_len, pulses, bins_dev, k_block,
-    after_ref, w_ref, chirp_ref,
+    facet_n, pulse_n, order, share, group_len, pulses, k_block, after_ref, w_ref,
 ):
     mine_f, mine_z = lax.axis_index("facet"), lax.axis_index("pulse")
     k_ids = mine_f * k_block + lax.broadcasted_iota(jnp.int32, (k_block, LANES), 0)
@@ -376,6 +387,10 @@
     for at, (real, imag) in wide.items():
         w_ref[:k_block, at * LANES : at * LANES + LANES] = real.astype(bf16)
         w_ref[k_block:, at * LANES : at * LANES + LANES] = imag.astype(bf16)
+
+
+def chirp_kernel(pulses, bins_dev, k_block, after_ref, chirp_ref):
+    mine_f, mine_z = lax.axis_index("facet"), lax.axis_index("pulse")
     offset = mine_f * k_block - pulses // 2 + lax.broadcasted_iota(jnp.int32, (k_block, bins_dev), 0)
     bins = mine_z * bins_dev + lax.broadcasted_iota(jnp.int32, (k_block, bins_dev), 1)
     phase = (offset * offset).astype(f32) * (8.0 / (2.0 * pulses)) / (8.0 + bins.astype(f32))
@@ -384,32 +399,41 @@
     chirp_ref[1] = sine
 
 
-def transform_tables(after, facet_n, pulse_n, order, share, group_len, pulses, bins_dev, k_block):
+def transform_tables(after, *sizes):
+    pulses, k_block = sizes[-2:]
     return pl.pallas_call(
-        functools.partial(
-            transform_tables_kernel, facet_n, pulse_n, order, share, group_len, pulses, bins_dev, k_block
-        ),
-        out_shape=(
-            jax.ShapeDtypeStruct((2 * k_block, pulses), bf16),
-            jax.ShapeDtypeStruct((2, k_block, bins_dev), f32),
-        ),
+        functools.partial(transform_tables_kernel, *sizes),
+        out_shape=jax.ShapeDtypeStruct((2 * k_block, pulses), bf16),
         in_specs=[pl.BlockSpec(memory_space=pl.ANY)],
-        out_specs=(pl.BlockSpec(memory_space=pltpu.VMEM),) * 2,
+        out_specs=pl.BlockSpec(memory_space=pltpu.VMEM),
         compiler_params=pltpu.CompilerParams(vmem_limit_bytes=16 << 20),
         name="transform_tables",
     )(after)
 
 
+def chirp_table(after, pulses, bins_dev, k_block):
+    return pl.pallas_call(
+        functools.partial(chirp_kernel, pulses, bins_dev, k_block),
+        out_shape=jax.ShapeDtypeStruct((2, k_block, bins_dev), f32),
+        in_specs=[pl.BlockSpec(memory_space=pl.ANY)],
+        out_specs=pl.BlockSpec(memory_space=pltpu.VMEM),
+        compiler_params=pltpu.CompilerParams(vmem_limit_bytes=16 << 20),
+        name="chirp_table",
+    )(after)
+
+
 def transform_kernel(places, has_total, k_block, bins_dev, w_ref, *refs):
     total = refs[0][...] if has_total else None
-    pieces = refs[has_total : has_total + len(places)]
-    for place, piece in zip(places, pieces):
+    end = has_total + 2 * len(places)
+    for i, place in enumerate(places):
+        at = has_total + 2 * i
+        piece = jnp.concatenate([refs[at][...], refs[at + 1][...]], axis=0)
         rows = piece.shape[0]
         part = jnp.dot(
-            w_ref[:, place * rows : place * rows + rows], piece[...], preferred_element_type=f32
+            w_ref[:, place * rows : place * rows + rows], piece, preferred_element_type=f32
         )
         total = part if total is None else total + part
-    rest = refs[has_total + len(places) :]
+    rest = refs[end:]
     if len(rest) == 1:
         rest[0][...] = total
         return
@@ -422,7 +446,9 @@
 
 
 def transform(w, total, pieces, places, k_block, bins_dev, chirp=None):
-    operands = [w] + ([] if total is None else [total]) + [pieces[at] for at in places]
+    operands = [w] + ([] if total is None else [total])
+    for at in places:
+        operands += pieces[at]
     shape = (2 * k_block, 2 * bins_dev)
     if chirp is not None:
         operands.append(chirp)
@@ -476,9 +502,8 @@
     fold = fold.reshape(2048, 256)
     echo = echoes(buildings, stations, fold, facets, blocks, groups, group_len)
     order = [1 << i for i in range(facet_n.bit_length() - 1)]
-    w, chirp = transform_tables(
-        echo, facet_n, pulse_n, order, share, group_len, pulses, bins_dev, k_block
-    )
+    w = transform_tables(echo, facet_n, pulse_n, order, share, group_len, pulses, k_block)
+    chirp = chirp_table(echo, pulses, bins_dev, k_block)
 
     echo = echo.reshape(QUADS, groups, 8, 2, LANES)[:, :, :group_len]
     if pulse_n > QUADS:
@@ -488,9 +513,10 @@
     for mask in range(1, pulse_n):
         piece = lax.dynamic_index_in_dim(echo, mine_z ^ mask, 0, keepdims=False)
         turned.append(swap(piece, "pulse", pulse_n, mask))
-    turned, w, chirp = lax.optimization_barrier((jnp.concatenate(turned), w, chirp))
-
-    pieces = gather_facet(turned, facet_n)
+
+    first = gather_facet(turned[0], facet_n)
+    rest = gather_facet(jnp.concatenate(turned[1:]), facet_n)
+    pieces = list(zip(first, rest))
     total = transform(w, None, pieces, [0, 1], k_block, bins_dev)
     total = transform(w, total, pieces, list(range(2, facet_n, 2)), k_block, bins_dev)
     return transform(w, total, pieces, list(range(3, facet_n, 2)), k_block, bins_dev, chirp)

time: 45.7 us -> 55 us (1.20)
  waiting for transfers between devices: 9.92 us -> 16.7 us
  starting transfers between devices: 16.8 us -> 19.2 us
    ppermute x17 -> x24, waiting for transfers between devices: 9.92 us -> 16.7 us  [swap(): return lax.ppermute(x, axis, [(i, i ^ mask) for i in range(size)])]
    ppermute x17 -> x24, starting transfers between devices: 16.8 us -> 19.2 us  [swap(): return lax.ppermute(x, axis, [(i, i ^ mask) for i in range(size)])]
    pallas_call x1 -> x2, Pallas kernels: 2 us -> 2.02 us  [the longest x1 1.87 us: transform_tables(): pl.pallas_call(functools.partial(transform_tables_kernel, *sizes), out_sh...]
  transfers between devices with their start and end apart: 17 -> 24, of which waited for: 9 -> 10; matrix products, arithmetic and copies ran while one was open for 2% -> 2% of each run, Pallas kernels for 6% -> 5%
where the time goes in v2:
time: 55 us; the launch traced here: 54.8 us
  starting transfers between devices  19.2 us (35%)
  Pallas kernels  17.6 us (32%)
  waiting for transfers between devices  16.7 us (30%)
  other arithmetic  0.92 us (2%)
    ppermute x24, starting transfers between devices, swap(): return lax.ppermute(x, axis, [(i, i ^ mask) for i in range(size)])  19.2 us
    ppermute x24, waiting for transfers between devices, swap(): return lax.ppermute(x, axis, [(i, i ^ mask) for i in range(size)])  16.7 us
    pallas_call x1, Pallas kernels, echoes(): pl.pallas_call(functools.partial(echo_kernel, pieces, blocks, groups, gro...  12.7 us
    pallas_call x1, Pallas kernels, transform_tables(): pl.pallas_call(functools.partial(transform_tables_kernel, *sizes), out_sh...  1.87 us
    pallas_call x3, Pallas kernels, transform(): pl.pallas_call(functools.partial(transform_kernel, places, total is not N...  1.86 us
  transfers between devices with their start and end apart: 24, of which 10 were waited for; matrix products, arithmetic and copies ran while one was open for 2% of the time, Pallas kernels for 5%

profile of v2, /device:TPU:0, one launch (start us, length us, event | category | flops | bytes accessed | tf_op | source)
XLA Modules:
  0.0 54.8 jit_solution(4304872630785926320)
XLA Ops:
  0.0 1.0 %pack_facets.1 = (f32[32,128]{1,0:T(8,128)S(1)}, f32[3,512]{1,0:T(4,128)S(1)}) custom-call(s32[6]{0:T(128)} %ids_hbm.1, f32[3,768]{1,0:T(4,128)} %positions_hbm.1, f32[2,768]{1,0:T(2,128)} %reflectivity_hbm.1, s32[12,16]{1,0:T(8,128)} %visible_hbm.1, f32[3,512]{1,0:T(4,128)} %platform_hbm.1), custom_call_target="tpu_custom_call" | custom-call | tf_op jit(solution)/shard_map/pack_facets/pallas_call | solution.py:330
  1.0 3.0 %collective-permute-start.1 = (f32[32,128]{1,0:T(8,128)S(1)}, f32[32,128]{1,0:T(8,128)S(1)}, u32[]{:S(2)}, u32[]{:S(2)}) collective-permute-start(f32[32,128]{1,0:T(8,128)S(1)} %get-tuple-element.8.refs_0_), channel_id=1, source_target_pairs={{0,8},{4,12},{8,0},{12,4},{16,24},{20,28},{24,16},{28,20},{1,9},{5... | collective-permute-start | bytes 49160 | tf_op jit(solution)/shard_map/ppermute | solution.py:468
  4.1 1.5 %collective-permute-start.3 = (f32[32,128]{1,0:T(8,128)S(1)}, f32[32,128]{1,0:T(8,128)S(1)}, u32[]{:S(2)}, u32[]{:S(2)}) collective-permute-start(f32[32,128]{1,0:T(8,128)S(1)} %get-tuple-element.8.refs_0_), channel_id=1, source_target_pairs={{0,16},{4,20},{8,24},{12,28},{16,0},{20,4},{24,8},{28,12},{1,17},{... | collective-permute-start | bytes 49160 | tf_op jit(solution)/shard_map/ppermute | solution.py:468
  5.6 0.0 collective-permute-start.5
  5.6 0.0 collective-permute-start
  5.6 0.9 %broadcast_multiply_fusion = bf16[256,256]{1,0:T(8,128)(2,1)S(1)} fusion(bf16[256,256]{1,0:T(8,128)(2,1)} %constant.30.clone, bf16[]{:T(256)S(6)} %convert_element_type.3), kind=kLoop, calls=%fused_computation.1 | loop fusion | flops 65536 | bytes 262146 | tf_op jit(solution)/shard_map/mul | solution.py:501
  6.5 0.0 collective-permute-done.1.refs_2_
  6.5 0.6 %collective-permute-start.2 = (f32[32,128]{1,0:T(8,128)S(1)}, f32[32,128]{1,0:T(8,128)S(1)}, u32[]{:S(2)}, u32[]{:S(2)}) collective-permute-start(f32[32,128]{1,0:T(8,128)S(1)} %collective-permute-done.1.refs_2_), channel_id=1, source_target_pairs={{0,4},{4,0},{8,12},{12,8},{16,20},{20,16},{24,28},{28,24},{1,5},{5... | collective-permute-start | bytes 49160 | tf_op jit(solution)/shard_map/ppermute | solution.py:468
  7.1 0.7 %collective-permute-done.3.refs_4_ = f32[32,128]{1,0:T(8,128)S(1)} collective-permute-done((f32[32,128]{1,0:T(8,128)S(1)}, f32[32,128]{1,0:T(8,128)S(1)}, u32[]{:S(2)}, u32[]{:S(2)}) %collective-permute-start.3) | collective-permute-done | bytes 16416 | tf_op jit(solution)/shard_map/ppermute | solution.py:468
  7.8 0.0 collective-permute-start.4
  7.8 2.4 %collective-permute-done.5.refs_6_ = f32[32,128]{1,0:T(8,128)S(1)} collective-permute-done((f32[32,128]{1,0:T(8,128)S(1)}, f32[32,128]{1,0:T(8,128)S(1)}, u32[]{:S(2)}, u32[]{:S(2)}) %collective-permute-start.5) | collective-permute-done | bytes 16416 | tf_op jit(solution)/shard_map/ppermute | solution.py:468
  10.2 0.0 collective-permute-start.6
  10.2 0.1 broadcast_bitcast_fusion.fold
  10.4 0.0 collective-permute-done.refs_1_
  10.4 0.0 collective-permute-done.2.refs_3_
  10.4 0.0 collective-permute-done.4.refs_5_
  10.4 1.0 %collective-permute-done.6.refs_7_ = f32[32,128]{1,0:T(8,128)S(1)} collective-permute-done((f32[32,128]{1,0:T(8,128)S(1)}, f32[32,128]{1,0:T(8,128)S(1)}, u32[]{:S(2)}, u32[]{:S(2)}) %collective-permute-start.6) | collective-permute-done | bytes 16416 | tf_op jit(solution)/shard_map/ppermute | solution.py:468
  11.4 12.7 %echoes.1.after_ref = bf16[4,64,256]{2,1,0:T(8,128)(2,1)S(1)} custom-call(f32[3,512]{1,0:T(4,128)S(1)} %get-tuple-element.7.platform_ref, bf16[2048,256]{1,0:T(8,128)(2,1)S(1)} %broadcast_bitcast_fusion.fold, f32[32,128]{1,0:T(8,128)S(1)} %get-tuple-element.8.refs_0_, f32[32,128]{1,0:T(8,128)S(1)} %collective-permute-done.refs_1_, ...), custom_call_target="tpu_custom_call" | custom-call | tf_op jit(solution)/shard_map/echoes/pallas_call | solution.py:262
  24.1 5.2 %collective-permute-start.7 = (bf16[64,256]{1,0:T(8,128)(2,1)S(1)}, bf16[64,256]{1,0:T(8,128)(2,1)S(1)}, u32[]{:S(2)}, u32[]{:S(2)}) collective-permute-start(bf16[64,256]{1,0:T(8,128)(2,1)S(1)} %get-tuple-element.11), channel_id=1, source_target_pairs={{0,1},{1,0},{2,3},{3,2},{4,5},{5,4},{6,7},{7,6},{8,9},{9,8},{10,11... | collective-permute-start | bytes 98312 | tf_op jit(solution)/shard_map/ppermute | solution.py:468
  29.3 0.6 %collective-permute-start.8 = (bf16[64,256]{1,0:T(8,128)(2,1)S(1)}, bf16[64,256]{1,0:T(8,128)(2,1)S(1)}, u32[]{:S(2)}, u32[]{:S(2)}) collective-permute-start(bf16[64,256]{1,0:T(8,128)(2,1)S(1)} %get-tuple-element.10), channel_id=1, source_target_pairs={{0,2},{1,3},{2,0},{3,1},{4,6},{5,7},{6,4},{7,5},{8,10},{9,11},{10,... | collective-permute-start | bytes 98312 | tf_op jit(solution)/shard_map/ppermute | solution.py:468
  29.9 1.8 %collective-permute-start.9 = (bf16[64,256]{1,0:T(8,128)(2,1)S(1)}, bf16[64,256]{1,0:T(8,128)(2,1)S(1)}, u32[]{:S(2)}, u32[]{:S(2)}) collective-permute-start(bf16[64,256]{1,0:T(8,128)(2,1)S(1)} %get-tuple-element.9), channel_id=1, source_target_pairs={{0,3},{1,2},{2,1},{3,0},{4,7},{5,6},{6,5},{7,4},{8,11},{9,10},{10,... | collective-permute-start | bytes 98312 | tf_op jit(solution)/shard_map/ppermute | solution.py:468
  31.7 0.0 collective-permute-done.7
  31.7 2.8 %collective-permute-done.8 = bf16[64,256]{1,0:T(8,128)(2,1)S(1)} collective-permute-done((bf16[64,256]{1,0:T(8,128)(2,1)S(1)}, bf16[64,256]{1,0:T(8,128)(2,1)S(1)}, u32[]{:S(2)}, u32[]{:S(2)}) %collective-permute-start.8) | collective-permute-done | bytes 32800 | tf_op jit(solution)/shard_map/ppermute | solution.py:468
  34.6 1.1 %collective-permute-done.9 = bf16[64,256]{1,0:T(8,128)(2,1)S(1)} collective-permute-done((bf16[64,256]{1,0:T(8,128)(2,1)S(1)}, bf16[64,256]{1,0:T(8,128)(2,1)S(1)}, u32[]{:S(2)}, u32[]{:S(2)}) %collective-permute-start.9) | collective-permute-done | bytes 32800 | tf_op jit(solution)/shard_map/ppermute | solution.py:468
  35.7 0.6 %collective-permute-start.13 = (bf16[192,256]{1,0:T(8,128)(2,1)S(1)}, bf16[192,256]{1,0:T(8,128)(2,1)S(1)}, u32[]{:S(2)}, u32[]{:S(2)}) collective-permute-start(bf16[192,256]{1,0:T(8,128)(2,1)S(1)} %constant_dynamic-update-slice_fusion.refs_1_), channel_id=1, source_target_pairs={{0,8},{4,12},{8,0},{12,4},{16,24},{20,28},{24,16},{28,20},{1,9},{5... | collective-permute-start | bytes 294920 | tf_op jit(solution)/shard_map/ppermute | solution.py:468
  36.2 0.2 collective-permute-start.15
  36.4 2.7 %collective-permute-start.17 = (bf16[192,256]{1,0:T(8,128)(2,1)S(1)}, bf16[192,256]{1,0:T(8,128)(2,1)S(1)}, u32[]{:S(2)}, u32[]{:S(2)}) collective-permute-start(bf16[192,256]{1,0:T(8,128)(2,1)S(1)} %constant_dynamic-update-slice_fusion.refs_1_), channel_id=1, source_target_pairs={{0,24},{4,28},{8,16},{12,20},{16,8},{20,12},{24,0},{28,4},{1,25},{... | collective-permute-start | bytes 294920 | tf_op jit(solution)/shard_map/ppermute | solution.py:468
  39.1 0.0 collective-permute-start.10
  39.2 0.6 %collective-permute-start.12 = (bf16[64,256]{1,0:T(8,128)(2,1)S(1)}, bf16[64,256]{1,0:T(8,128)(2,1)S(1)}, u32[]{:S(2)}, u32[]{:S(2)}) collective-permute-start(bf16[64,256]{1,0:T(8,128)(2,1)S(1)} %get-tuple-element.12.refs_0_), channel_id=1, source_target_pairs={{0,8},{4,12},{8,0},{12,4},{16,24},{20,28},{24,16},{28,20},{1,9},{5... | collective-permute-start | bytes 98312 | tf_op jit(solution)/shard_map/ppermute | solution.py:468
  39.7 0.6 %collective-permute-done.10.refs_2_ = bf16[64,256]{1,0:T(8,128)(2,1)S(1)} collective-permute-done((bf16[64,256]{1,0:T(8,128)(2,1)S(1)}, bf16[64,256]{1,0:T(8,128)(2,1)S(1)}, u32[]{:S(2)}, u32[]{:S(2)}) %collective-permute-start.10) | collective-permute-done | bytes 32800 | tf_op jit(solution)/shard_map/ppermute | solution.py:468
  40.4 0.3 collective-permute-start.14
  40.6 2.5 %collective-permute-done.12.refs_1_ = bf16[64,256]{1,0:T(8,128)(2,1)S(1)} collective-permute-done((bf16[64,256]{1,0:T(8,128)(2,1)S(1)}, bf16[64,256]{1,0:T(8,128)(2,1)S(1)}, u32[]{:S(2)}, u32[]{:S(2)}) %collective-permute-start.12) | collective-permute-done | bytes 32800 | tf_op jit(solution)/shard_map/ppermute | solution.py:468
  43.1 0.0 collective-permute-start.11
  43.1 1.2 %collective-permute-done.14.refs_3_ = bf16[64,256]{1,0:T(8,128)(2,1)S(1)} collective-permute-done((bf16[64,256]{1,0:T(8,128)(2,1)S(1)}, bf16[64,256]{1,0:T(8,128)(2,1)S(1)}, u32[]{:S(2)}, u32[]{:S(2)}) %collective-permute-start.14) | collective-permute-done | bytes 32800 | tf_op jit(solution)/shard_map/ppermute | solution.py:468
  44.3 1.1 %collective-permute-start.16 = (bf16[64,256]{1,0:T(8,128)(2,1)S(1)}, bf16[64,256]{1,0:T(8,128)(2,1)S(1)}, u32[]{:S(2)}, u32[]{:S(2)}) collective-permute-start(bf16[64,256]{1,0:T(8,128)(2,1)S(1)} %get-tuple-element.12.refs_0_), channel_id=1, source_target_pairs={{0,24},{4,28},{8,16},{12,20},{16,8},{20,12},{24,0},{28,4},{1,25},{... | collective-permute-start | bytes 98312 | tf_op jit(solution)/shard_map/ppermute | solution.py:468
  45.4 0.0 collective-permute-done.13.refs_2_
  45.4 0.0 collective-permute-start.19
  45.4 0.0 collective-permute-done.15.refs_4_
  45.4 0.5 collective-permute-start.21
  45.9 0.0 collective-permute-done.17.refs_6_
  45.9 0.1 collective-permute-start.23
  46.0 3.1 %collective-permute-done.16.refs_5_ = bf16[64,256]{1,0:T(8,128)(2,1)S(1)} collective-permute-done((bf16[64,256]{1,0:T(8,128)(2,1)S(1)}, bf16[64,256]{1,0:T(8,128)(2,1)S(1)}, u32[]{:S(2)}, u32[]{:S(2)}) %collective-permute-start.16) | collective-permute-done | bytes 32800 | tf_op jit(solution)/shard_map/ppermute | solution.py:468
  49.1 0.0 collective-permute-start.18
  49.1 1.2 %collective-permute-done.18.refs_1_ = bf16[64,256]{1,0:T(8,128)(2,1)S(1)} collective-permute-done((bf16[64,256]{1,0:T(8,128)(2,1)S(1)}, bf16[64,256]{1,0:T(8,128)(2,1)S(1)}, u32[]{:S(2)}, u32[]{:S(2)}) %collective-permute-start.18) | collective-permute-done | bytes 32800 | tf_op jit(solution)/shard_map/ppermute | solution.py:468
  50.3 0.2 collective-permute-start.20
  50.5 0.0 collective-permute-done.11.refs_3_
  50.5 0.3 collective-permute-start.22
  50.8 1.9 %transform_tables.1.w_ref = bf16[512,2048]{1,0:T(8,128)(2,1)S(1)} custom-call(bf16[4,64,256]{2,1,0:T(8,128)(2,1)S(1)} %echoes.1.after_ref), custom_call_target="tpu_custom_call" | custom-call | tf_op jit(solution)/shard_map/transform_tables/pallas_call | solution.py:404
  52.7 0.2 chirp_table.1.refs_7_
  52.8 0.3 transform.3.refs_0_
  53.2 0.4 transform.4.refs_0_
  53.5 0.0 collective-permute-done.20.refs_3_
  53.5 0.0 collective-permute-done.22.refs_5_
  53.6 0.0 collective-permute-done.19.refs_2_
  53.6 0.0 collective-permute-done.21.refs_4_
  53.6 0.0 collective-permute-done.23.refs_6_
  53.6 1.2 %transform.5 = f32[2,128,256]{2,1,0:T(8,128)} custom-call(bf16[512,2048]{1,0:T(8,128)(2,1)S(1)} %transform_tables.1.w_ref, f32[512,256]{1,0:T(8,128)S(1)} %transform.4.refs_0_, bf16[64,256]{1,0:T(8,128)(2,1)S(1)} %collective-permute-done.18.refs_1_, bf16[192,256]{1,0:T(8,128)(2,1)S(1)} %collective-permute-done.19.refs_2_, ...), custom_call_target="tpu_custom_call" | custom-call | tf_op jit(solution)/shard_map/transform/pallas_call | solution.py:457
  (4 shorter events, 0.0 us)
Async XLA Ops:
  1.0 5.5 %collective-permute-start.1 = (f32[32,128]{1,0:T(8,128)S(1)}, f32[32,128]{1,0:T(8,128)S(1)}, u32[]{:S(2)}, u32[]{:S(2)}) collective-permute-start(f32[32,128]{1,0:T(8,128)S(1)} %get-tuple-element.8.refs_0_), channel_id=1, source_target_pairs={{0,8},{4,12},{8,0},{12,4},{16,24},{20,28},{24,16},{28,20},{1,9},{5... | collective-permute-start | bytes 49160 | tf_op jit(solution)/shard_map/ppermute | solution.py:468
  4.1 3.7 %collective-permute-start.3 = (f32[32,128]{1,0:T(8,128)S(1)}, f32[32,128]{1,0:T(8,128)S(1)}, u32[]{:S(2)}, u32[]{:S(2)}) collective-permute-start(f32[32,128]{1,0:T(8,128)S(1)} %get-tuple-element.8.refs_0_), channel_id=1, source_target_pairs={{0,16},{4,20},{8,24},{12,28},{16,0},{20,4},{24,8},{28,12},{1,17},{... | collective-permute-start | bytes 49160 | tf_op jit(solution)/shard_map/ppermute | solution.py:468
  5.6 4.6 %collective-permute-start.5 = (f32[32,128]{1,0:T(8,128)S(1)}, f32[32,128]{1,0:T(8,128)S(1)}, u32[]{:S(2)}, u32[]{:S(2)}) collective-permute-start(f32[32,128]{1,0:T(8,128)S(1)} %get-tuple-element.8.refs_0_), channel_id=1, source_target_pairs={{0,24},{4,28},{8,16},{12,20},{16,8},{20,12},{24,0},{28,4},{1,25},{... | collective-permute-start | bytes 49160 | tf_op jit(solution)/shard_map/ppermute | solution.py:468
  5.6 4.8 %collective-permute-start = (f32[32,128]{1,0:T(8,128)S(1)}, f32[32,128]{1,0:T(8,128)S(1)}, u32[]{:S(2)}, u32[]{:S(2)}) collective-permute-start(f32[32,128]{1,0:T(8,128)S(1)} %get-tuple-element.8.refs_0_), channel_id=1, source_target_pairs={{0,4},{4,0},{8,12},{12,8},{16,20},{20,16},{24,28},{28,24},{1,5},{5... | collective-permute-start | bytes 49160 | tf_op jit(solution)/shard_map/ppermute | solution.py:468
  6.5 3.9 %collective-permute-start.2 = (f32[32,128]{1,0:T(8,128)S(1)}, f32[32,128]{1,0:T(8,128)S(1)}, u32[]{:S(2)}, u32[]{:S(2)}) collective-permute-start(f32[32,128]{1,0:T(8,128)S(1)} %collective-permute-done.1.refs_2_), channel_id=1, source_target_pairs={{0,4},{4,0},{8,12},{12,8},{16,20},{20,16},{24,28},{28,24},{1,5},{5... | collective-permute-start | bytes 49160 | tf_op jit(solution)/shard_map/ppermute | solution.py:468
  7.8 2.6 %collective-permute-start.4 = (f32[32,128]{1,0:T(8,128)S(1)}, f32[32,128]{1,0:T(8,128)S(1)}, u32[]{:S(2)}, u32[]{:S(2)}) collective-permute-start(f32[32,128]{1,0:T(8,128)S(1)} %collective-permute-done.3.refs_4_), channel_id=1, source_target_pairs={{0,4},{4,0},{8,12},{12,8},{16,20},{20,16},{24,28},{28,24},{1,5},{5... | collective-permute-start | bytes 49160 | tf_op jit(solution)/shard_map/ppermute | solution.py:468
  10.2 1.2 %collective-permute-start.6 = (f32[32,128]{1,0:T(8,128)S(1)}, f32[32,128]{1,0:T(8,128)S(1)}, u32[]{:S(2)}, u32[]{:S(2)}) collective-permute-start(f32[32,128]{1,0:T(8,128)S(1)} %collective-permute-done.5.refs_6_), channel_id=1, source_target_pairs={{0,4},{4,0},{8,12},{12,8},{16,20},{20,16},{24,28},{28,24},{1,5},{5... | collective-permute-start | bytes 49160 | tf_op jit(solution)/shard_map/ppermute | solution.py:468
  24.1 7.6 %collective-permute-start.7 = (bf16[64,256]{1,0:T(8,128)(2,1)S(1)}, bf16[64,256]{1,0:T(8,128)(2,1)S(1)}, u32[]{:S(2)}, u32[]{:S(2)}) collective-permute-start(bf16[64,256]{1,0:T(8,128)(2,1)S(1)} %get-tuple-element.11), channel_id=1, source_target_pairs={{0,1},{1,0},{2,3},{3,2},{4,5},{5,4},{6,7},{7,6},{8,9},{9,8},{10,11... | collective-permute-start | bytes 98312 | tf_op jit(solution)/shard_map/ppermute | solution.py:468
  29.3 5.3 %collective-permute-start.8 = (bf16[64,256]{1,0:T(8,128)(2,1)S(1)}, bf16[64,256]{1,0:T(8,128)(2,1)S(1)}, u32[]{:S(2)}, u32[]{:S(2)}) collective-permute-start(bf16[64,256]{1,0:T(8,128)(2,1)S(1)} %get-tuple-element.10), channel_id=1, source_target_pairs={{0,2},{1,3},{2,0},{3,1},{4,6},{5,7},{6,4},{7,5},{8,10},{9,11},{10,... | collective-permute-start | bytes 98312 | tf_op jit(solution)/shard_map/ppermute | solution.py:468
  29.9 5.7 %collective-permute-start.9 = (bf16[64,256]{1,0:T(8,128)(2,1)S(1)}, bf16[64,256]{1,0:T(8,128)(2,1)S(1)}, u32[]{:S(2)}, u32[]{:S(2)}) collective-permute-start(bf16[64,256]{1,0:T(8,128)(2,1)S(1)} %get-tuple-element.9), channel_id=1, source_target_pairs={{0,3},{1,2},{2,1},{3,0},{4,7},{5,6},{6,5},{7,4},{8,11},{9,10},{10,... | collective-permute-start | bytes 98312 | tf_op jit(solution)/shard_map/ppermute | solution.py:468
  35.7 9.7 %collective-permute-start.13 = (bf16[192,256]{1,0:T(8,128)(2,1)S(1)}, bf16[192,256]{1,0:T(8,128)(2,1)S(1)}, u32[]{:S(2)}, u32[]{:S(2)}) collective-permute-start(bf16[192,256]{1,0:T(8,128)(2,1)S(1)} %constant_dynamic-update-slice_fusion.refs_1_), channel_id=1, source_target_pairs={{0,8},{4,12},{8,0},{12,4},{16,24},{20,28},{24,16},{28,20},{1,9},{5... | collective-permute-start | bytes 294920 | tf_op jit(solution)/shard_map/ppermute | solution.py:468
  36.2 9.2 %collective-permute-start.15 = (bf16[192,256]{1,0:T(8,128)(2,1)S(1)}, bf16[192,256]{1,0:T(8,128)(2,1)S(1)}, u32[]{:S(2)}, u32[]{:S(2)}) collective-permute-start(bf16[192,256]{1,0:T(8,128)(2,1)S(1)} %constant_dynamic-update-slice_fusion.refs_1_), channel_id=1, source_target_pairs={{0,16},{4,20},{8,24},{12,28},{16,0},{20,4},{24,8},{28,12},{1,17},{... | collective-permute-start | bytes 294920 | tf_op jit(solution)/shard_map/ppermute | solution.py:468
  36.4 9.5 %collective-permute-start.17 = (bf16[192,256]{1,0:T(8,128)(2,1)S(1)}, bf16[192,256]{1,0:T(8,128)(2,1)S(1)}, u32[]{:S(2)}, u32[]{:S(2)}) collective-permute-start(bf16[192,256]{1,0:T(8,128)(2,1)S(1)} %constant_dynamic-update-slice_fusion.refs_1_), channel_id=1, source_target_pairs={{0,24},{4,28},{8,16},{12,20},{16,8},{20,12},{24,0},{28,4},{1,25},{... | collective-permute-start | bytes 294920 | tf_op jit(solution)/shard_map/ppermute | solution.py:468
  39.1 1.2 %collective-permute-start.10 = (bf16[64,256]{1,0:T(8,128)(2,1)S(1)}, bf16[64,256]{1,0:T(8,128)(2,1)S(1)}, u32[]{:S(2)}, u32[]{:S(2)}) collective-permute-start(bf16[64,256]{1,0:T(8,128)(2,1)S(1)} %get-tuple-element.12.refs_0_), channel_id=1, source_target_pairs={{0,4},{4,0},{8,12},{12,8},{16,20},{20,16},{24,28},{28,24},{1,5},{5... | collective-permute-start | bytes 98312 | tf_op jit(solution)/shard_map/ppermute | solution.py:468
  39.2 3.9 %collective-permute-start.12 = (bf16[64,256]{1,0:T(8,128)(2,1)S(1)}, bf16[64,256]{1,0:T(8,128)(2,1)S(1)}, u32[]{:S(2)}, u32[]{:S(2)}) collective-permute-start(bf16[64,256]{1,0:T(8,128)(2,1)S(1)} %get-tuple-element.12.refs_0_), channel_id=1, source_target_pairs={{0,8},{4,12},{8,0},{12,4},{16,24},{20,28},{24,16},{28,20},{1,9},{5... | collective-permute-start | bytes 98312 | tf_op jit(solution)/shard_map/ppermute | solution.py:468
  40.4 3.9 %collective-permute-start.14 = (bf16[64,256]{1,0:T(8,128)(2,1)S(1)}, bf16[64,256]{1,0:T(8,128)(2,1)S(1)}, u32[]{:S(2)}, u32[]{:S(2)}) collective-permute-start(bf16[64,256]{1,0:T(8,128)(2,1)S(1)} %get-tuple-element.12.refs_0_), channel_id=1, source_target_pairs={{0,16},{4,20},{8,24},{12,28},{16,0},{20,4},{24,8},{28,12},{1,17},{... | collective-permute-start | bytes 98312 | tf_op jit(solution)/shard_map/ppermute | solution.py:468
  43.1 7.4 %collective-permute-start.11 = (bf16[192,256]{1,0:T(8,128)(2,1)S(1)}, bf16[192,256]{1,0:T(8,128)(2,1)S(1)}, u32[]{:S(2)}, u32[]{:S(2)}) collective-permute-start(bf16[192,256]{1,0:T(8,128)(2,1)S(1)} %constant_dynamic-update-slice_fusion.refs_1_), channel_id=1, source_target_pairs={{0,4},{4,0},{8,12},{12,8},{16,20},{20,16},{24,28},{28,24},{1,5},{5... | collective-permute-start | bytes 294920 | tf_op jit(solution)/shard_map/ppermute | solution.py:468
  44.3 4.8 %collective-permute-start.16 = (bf16[64,256]{1,0:T(8,128)(2,1)S(1)}, bf16[64,256]{1,0:T(8,128)(2,1)S(1)}, u32[]{:S(2)}, u32[]{:S(2)}) collective-permute-start(bf16[64,256]{1,0:T(8,128)(2,1)S(1)} %get-tuple-element.12.refs_0_), channel_id=1, source_target_pairs={{0,24},{4,28},{8,16},{12,20},{16,8},{20,12},{24,0},{28,4},{1,25},{... | collective-permute-start | bytes 98312 | tf_op jit(solution)/shard_map/ppermute | solution.py:468
  45.4 8.2 %collective-permute-start.19 = (bf16[192,256]{1,0:T(8,128)(2,1)S(1)}, bf16[192,256]{1,0:T(8,128)(2,1)S(1)}, u32[]{:S(2)}, u32[]{:S(2)}) collective-permute-start(bf16[192,256]{1,0:T(8,128)(2,1)S(1)} %collective-permute-done.13.refs_2_), channel_id=1, source_target_pairs={{0,4},{4,0},{8,12},{12,8},{16,20},{20,16},{24,28},{28,24},{1,5},{5... | collective-permute-start | bytes 294920 | tf_op jit(solution)/shard_map/ppermute | solution.py:468
  45.4 8.2 %collective-permute-start.21 = (bf16[192,256]{1,0:T(8,128)(2,1)S(1)}, bf16[192,256]{1,0:T(8,128)(2,1)S(1)}, u32[]{:S(2)}, u32[]{:S(2)}) collective-permute-start(bf16[192,256]{1,0:T(8,128)(2,1)S(1)} %collective-permute-done.15.refs_4_), channel_id=1, source_target_pairs={{0,4},{4,0},{8,12},{12,8},{16,20},{20,16},{24,28},{28,24},{1,5},{5... | collective-permute-start | bytes 294920 | tf_op jit(solution)/shard_map/ppermute | solution.py:468
  45.9 7.7 %collective-permute-start.23 = (bf16[192,256]{1,0:T(8,128)(2,1)S(1)}, bf16[192,256]{1,0:T(8,128)(2,1)S(1)}, u32[]{:S(2)}, u32[]{:S(2)}) collective-permute-start(bf16[192,256]{1,0:T(8,128)(2,1)S(1)} %collective-permute-done.17.refs_6_), channel_id=1, source_target_pairs={{0,4},{4,0},{8,12},{12,8},{16,20},{20,16},{24,28},{28,24},{1,5},{5... | collective-permute-start | bytes 294920 | tf_op jit(solution)/shard_map/ppermute | solution.py:468
  49.1 1.2 %collective-permute-start.18 = (bf16[64,256]{1,0:T(8,128)(2,1)S(1)}, bf16[64,256]{1,0:T(8,128)(2,1)S(1)}, u32[]{:S(2)}, u32[]{:S(2)}) collective-permute-start(bf16[64,256]{1,0:T(8,128)(2,1)S(1)} %collective-permute-done.12.refs_1_), channel_id=1, source_target_pairs={{0,4},{4,0},{8,12},{12,8},{16,20},{20,16},{24,28},{28,24},{1,5},{5... | collective-permute-start | bytes 98312 | tf_op jit(solution)/shard_map/ppermute | solution.py:468
  50.3 3.2 %collective-permute-start.20 = (bf16[64,256]{1,0:T(8,128)(2,1)S(1)}, bf16[64,256]{1,0:T(8,128)(2,1)S(1)}, u32[]{:S(2)}, u32[]{:S(2)}) collective-permute-start(bf16[64,256]{1,0:T(8,128)(2,1)S(1)} %collective-permute-done.14.refs_3_), channel_id=1, source_target_pairs={{0,4},{4,0},{8,12},{12,8},{16,20},{20,16},{24,28},{28,24},{1,5},{5... | collective-permute-start | bytes 98312 | tf_op jit(solution)/shard_map/ppermute | solution.py:468
  50.5 3.1 %collective-permute-start.22 = (bf16[64,256]{1,0:T(8,128)(2,1)S(1)}, bf16[64,256]{1,0:T(8,128)(2,1)S(1)}, u32[]{:S(2)}, u32[]{:S(2)}) collective-permute-start(bf16[64,256]{1,0:T(8,128)(2,1)S(1)} %collective-permute-done.16.refs_5_), channel_id=1, source_target_pairs={{0,4},{4,0},{8,12},{12,8},{16,20},{20,16},{24,28},{28,24},{1,5},{5... | collective-permute-start | bytes 98312 | tf_op jit(solution)/shard_map/ppermute | solution.py:468
